TPU v7x, 512 devices: a whole 4x8x8 slice. The times are simulated.
512 devices in a mesh: tok: 32 (over y_hi, z, core), head: 16 (over y_lo, x).
Axes of the slice: x: 4, y: 8 (y_hi: 2, y_lo: 4; y = y_hi * 4 + y_lo), z: 8, core: 2. Of those that a mesh axis runs over, the one named last changes fastest.
Arguments:
- queries: bfloat16 [4096, 4096], P('tok', 'head'), may hold values from -512 to 512
- kv: bfloat16 [4, 4096, 128], P(None, 'tok', 'head'), may hold values from -6 to 6
- w_out: bfloat16 [4096, 8192], P('head', 'tok'), may hold values from -0.09375 to 0.09375
Outputs:
- projected: bfloat16 [4096, 8192], P('head', 'tok')
All inputs are finite; a program needn't handle non-finite values.
Results may differ from a plain program's by a relative error of at most 0.011.
Values may be sent and summed in bfloat16 or wider, within the bound.
No kernel may reach another device: no remote copies, remote signals or barrier semaphores. Data moves between devices by JAX's collectives and lax.ppermute only.
A program may use at most 64 MiB of HBM per device.

v0:
```python
import math

import jax
import jax.numpy as jnp
from jax import lax
from jax.sharding import PartitionSpec as P

HD = 128
W1 = 512
W2 = 32


def shifted(x, axis, by):
    count = lax.axis_size(axis)
    pairs = [(i, i + by) for i in range(count) if 0 <= i + by < count]
    return lax.ppermute(x, axis, pairs)


def attend_block(query_part, first_part, second_part, first_anchor, second_anchor):
    block_rows = query_part.shape[0]
    score_scale = 3.0 / math.sqrt(query_part.shape[-1])
    query_pos = jnp.arange(block_rows)[:, None]
    first_slot = jnp.arange(first_part.shape[1])[None, :]
    allowed_first = (
        (first_slot > query_pos) & (first_slot <= query_pos + W1) & (first_anchor + first_slot >= 0)
    )
    second_slot = jnp.arange(second_part.shape[1])[None, :]
    allowed_second = (
        (second_slot > query_pos)
        & (second_slot <= query_pos + W2)
        & (second_anchor + second_slot >= 0)
    )
    query_key = (
        query_part.astype(jnp.float32)[:, :, None, :]
        * second_part[0].astype(jnp.float32)[None, None, :, :]
    ).astype(jnp.bfloat16)
    pair_shape = query_key.shape[:3]
    flattened = query_key.reshape(-1, query_key.shape[-1])
    scores = jnp.dot(flattened, first_part[0].T, preferred_element_type=jnp.float32)
    scores = scores.reshape(pair_shape + (first_part.shape[1],)) * score_scale
    allowed = allowed_second[:, None, :, None] & allowed_first[:, None, None, :]
    scores = jnp.where(allowed, scores, -jnp.inf)
    row_max = jnp.max(scores, axis=(2, 3), keepdims=True)
    exponent = jnp.exp(scores - row_max)
    denominator = jnp.sum(exponent, axis=(2, 3))
    weights = exponent.astype(jnp.bfloat16)
    value_mix = jnp.dot(
        weights.reshape(-1, first_part.shape[1]), first_part[1], preferred_element_type=jnp.float32
    )
    value_mix = value_mix.reshape(pair_shape + (first_part.shape[2],))
    attended = jnp.sum(value_mix * second_part[1].astype(jnp.float32)[None, None, :, :], axis=2)
    return (attended / denominator[:, :, None]).astype(jnp.bfloat16)


def body(queries, kv, w_out):
    local_rows = queries.shape[0]
    local_heads = queries.shape[1] // HD
    shard_base = lax.axis_index("tok") * local_rows
    reach_count = max(W1 // local_rows, 1)
    features = lax.all_gather(kv, "head", axis=2, tiled=True)
    own_first = features[0:2]
    earlier = []
    for distance in range(reach_count, 0, -1):
        earlier.append(shifted(own_first, "tok", distance))
    first_keys = jnp.concatenate(earlier + [own_first], axis=1)
    near_tail = shifted(features[2:4, local_rows - W2 :], "tok", 1)
    second_keys = jnp.concatenate([near_tail, features[2:4]], axis=1)
    block_rows = math.gcd(32, local_rows)

    def block(block_index):
        offset = block_index * block_rows
        query_part = lax.dynamic_slice_in_dim(queries, offset, block_rows, 0).reshape(
            block_rows, local_heads, HD
        )
        first_part = lax.dynamic_slice_in_dim(first_keys, offset, W1 + block_rows, 1)
        second_part = lax.dynamic_slice_in_dim(second_keys, offset, W2 + block_rows, 1)
        attended = attend_block(
            query_part, first_part, second_part, shard_base + offset - W1, shard_base + offset - W2
        )
        return attended.reshape(block_rows, local_heads * HD)

    attention = lax.map(block, jnp.arange(local_rows // block_rows, dtype=jnp.int32)).reshape(
        local_rows, local_heads * HD
    )
    every_token = lax.all_gather(attention, "tok", axis=0, tiled=True)
    gathered_rows = lax.all_to_all(every_token, "head", split_axis=0, concat_axis=1, tiled=True)
    summed = jnp.dot(
        gathered_rows,
        lax.all_gather(w_out, "head", axis=0, tiled=True),
        preferred_element_type=jnp.float32,
    )
    return summed.astype(jnp.bfloat16)


def solution(mesh):
    return jax.shard_map(
        body,
        mesh=mesh,
        in_specs=(P("tok", "head"), P(None, "tok", "head"), P("head", "tok")),
        out_specs=P("head", "tok"),
        check_vma=False,
    )
```

profile of v0, /device:TPU:126, one launch (start us, length us, event | category | flops | bytes accessed | tf_op | source)
XLA Modules:
  0.0 317.6 jit_solution(5996668151703882801)
XLA Ops:
  7.4 0.7 copy.8
  8.1 37.1 %all_gather.9 = bf16[4,128,128]{1,0,2:T(4,128)(2,1)S(1)} all-gather(bf16[4,128,8]{1,0,2:T(4,128)(2,1)S(1)} %copy.8), channel_id=1, replica_groups=mesh['tok'=32,'head'=16] {'head'}, dimensions={2}, use_global_device_ids=true | all-gather | bytes 139264 | tf_op jit(solution)/shard_map/all_gather | solution.py:60
  45.2 6.1 %collective-permute-start.1 = (bf16[2,128,128]{1,0,2:T(2,128)(2,1)S(1)}, bf16[2,128,128]{1,0,2:T(2,128)(2,1)S(1)}, u32[]{:S(2)}, u32[]{:S(2)}) collective-permute-start(bf16[2,128,128]{1,0,2:T(2,128)(2,1)S(1)} %slice.38), channel_id=1, source_target_pairs={{0,64},{16,80},{32,96},{48,112},{64,128},{80,144},{96,160},{112,17... | collective-permute-start | bytes 196616 | tf_op jit(solution)/shard_map/ppermute | solution.py:16
  51.3 1.9 collective-permute-start.2
  53.3 5.5 %collective-permute-start.3 = (bf16[2,128,128]{1,0,2:T(2,128)(2,1)S(1)}, bf16[2,128,128]{1,0,2:T(2,128)(2,1)S(1)}, u32[]{:S(2)}, u32[]{:S(2)}) collective-permute-start(bf16[2,128,128]{1,0,2:T(2,128)(2,1)S(1)} %slice.38), channel_id=1, source_target_pairs={{0,32},{16,48},{32,64},{48,80},{64,96},{80,112},{96,128},{112,144}... | collective-permute-start | bytes 196616 | tf_op jit(solution)/shard_map/ppermute | solution.py:16
  58.8 4.1 %collective-permute-start.4 = (bf16[2,128,128]{1,0,2:T(2,128)(2,1)S(1)}, bf16[2,128,128]{1,0,2:T(2,128)(2,1)S(1)}, u32[]{:S(2)}, u32[]{:S(2)}) collective-permute-start(bf16[2,128,128]{1,0,2:T(2,128)(2,1)S(1)} %slice.38), channel_id=1, source_target_pairs={{0,16},{16,32},{32,48},{48,64},{64,80},{80,96},{96,112},{112,128},... | collective-permute-start | bytes 196616 | tf_op jit(solution)/shard_map/ppermute | solution.py:16
  62.9 0.1 slice.36
  63.0 1.9 collective-permute-start
  65.1 0.1 constant_dynamic-update-slice_fusion.4
  65.2 0.1 constant_dynamic-update-slice_fusion.3
  65.3 0.1 constant_dynamic-update-slice_fusion.2
  65.4 0.1 constant_dynamic-update-slice_fusion.1
  65.5 3.1 collective-permute-done
  68.6 0.3 pad_maximum_fusion
  68.9 0.1 copy.9
  69.0 0.7 copy.10
  69.7 46.2 %while.12 = (s32[]{:T(128)}, bf16[4,32,256]{2,1,0:T(8,128)(2,1)S(1)}, s32[4]{0:T(128)S(1)}, s32[]{:T(128)}, bf16[128,256]{1,0:T(8,128)(2,1)}, /*index=5*/bf16[2,...) while((s32[]{:T(128)}, ...), condition=%wide.region_4.5_spmd, body=%wide.region_0.4_spmd.sunk | while | flops 1168684288 | bytes 33956884 | solution.py:82
  69.7 0.6 dynamic_slice.29
  71.0 0.7 dynamic-slice_convert_fusion.2
  71.8 0.1 fusion.30
  71.9 0.1 fusion.31
  72.0 0.8 broadcast_and_fusion.2
  72.8 2.1 fusion.33
  74.9 3.1 fusion.34
  78.0 3.0 multiply_reduce_fusion.2
  81.1 0.1 divide_convert_fusion.2
  81.2 0.6 dynamic_slice.29
  82.5 0.7 dynamic-slice_convert_fusion.2
  83.3 0.1 fusion.30
  83.4 0.1 fusion.31
  83.5 0.8 broadcast_and_fusion.2
  84.4 2.1 fusion.33
  86.5 3.1 fusion.34
  89.6 3.0 multiply_reduce_fusion.2
  92.6 0.1 divide_convert_fusion.2
  92.8 0.6 dynamic_slice.29
  94.1 0.7 dynamic-slice_convert_fusion.2
  94.9 0.1 fusion.30
  95.0 0.1 fusion.31
  95.1 0.8 broadcast_and_fusion.2
  95.9 2.1 fusion.33
  98.0 3.1 fusion.34
  101.1 3.0 multiply_reduce_fusion.2
  104.2 0.1 divide_convert_fusion.2
  104.3 0.6 dynamic_slice.29
  105.6 0.7 dynamic-slice_convert_fusion.2
  106.4 0.1 fusion.30
  106.5 0.1 fusion.31
  106.6 0.8 broadcast_and_fusion.2
  107.4 2.1 fusion.33
  109.5 3.1 fusion.34
  112.7 3.0 multiply_reduce_fusion.2
  115.7 0.1 divide_convert_fusion.2
  115.9 0.0 copy-start
  115.9 0.6 copy-done
  116.5 0.0 all-gather.3.cloned.1.call-update
  116.5 89.8 %all-gather.3.cloned.1.call-done = bf16[4096,256]{1,0:T(8,128)(2,1)} async-done(((bf16[128,256]{1,0:T(8,128)(2,1)}), bf16[4096,256]{1,0:T(8,128)(2,1)}) %all-gather.3.cloned.1.call-update) | async-done | bytes 2097168 | tf_op jit(solution)/shard_map/all_gather | solution.py:85
  206.4 10.0 %all-to-all-start = ((bf16[16,256,256]{2,1,0:T(8,128)(2,1)}), bf16[16,256,256]{2,1,0:T(8,128)(2,1)S(1)}, u32[]{:S(2)}, u32[]{:S(2)}) async-start(bf16[16,256,256]{2,1,0:T(8,128)(2,1)} %bitcast.42), calls=%async_computation | async-start | bytes 4194304 | tf_op jit(solution)/shard_map/all_to_all | solution.py:86
  216.4 0.0 all-gather.5.cloned.1.call-start
  216.5 0.5 all-gather.5.cloned.1.call-update
  217.0 57.8 %all-to-all-done = bf16[16,256,256]{2,1,0:T(8,128)(2,1)S(1)} async-done(((bf16[16,256,256]{2,1,0:T(8,128)(2,1)}), bf16[16,256,256]{2,1,0:T(8,128)(2,1)S(1)}, u32[]{:S(2)}, u32[]{:S(2)}) %all-to-all-start) | async-done | bytes 2097184 | tf_op jit(solution)/shard_map/all_to_all | solution.py:86
  274.8 2.4 copy.11
  277.1 29.3 %all-gather.5.cloned.1.call-done = bf16[4096,256]{1,0:T(8,128)(2,1)} async-done(((bf16[256,256]{1,0:T(8,128)(2,1)}), bf16[4096,256]{1,0:T(8,128)(2,1)}) %all-gather.5.cloned.1.call-update) | async-done | bytes 2097168 | tf_op jit(solution)/shard_map/all_gather | solution.py:89
  306.5 3.6 %convolution_convert_fusion = bf16[256,256]{1,0:T(8,128)(2,1)} fusion(bf16[256,4096]{0,1:T(8,128)(2,1)} %bitcast.43, bf16[4096,256]{1,0:T(8,128)(2,1)} %all-gather.5.cloned.1.call-done), kind=kOutput, calls=%fused_computation.38 | convolution fusion | flops 536936448 | bytes 4325376 | tf_op jit(solution)/shard_map/dot_general | solution.py:87
  (41 shorter events, 0.4 us)
Async XLA Ops:
  7.4 199.0 %all-gather.3.cloned.1.call-start = ((), (), s32[]{:S(2)}) async-start(), calls=%async_computation.1 | async-start | bytes 2162688 | tf_op jit(solution)/shard_map/all_gather | solution.py:85
  45.2 19.7 %collective-permute-start.1 = (bf16[2,128,128]{1,0,2:T(2,128)(2,1)S(1)}, bf16[2,128,128]{1,0,2:T(2,128)(2,1)S(1)}, u32[]{:S(2)}, u32[]{:S(2)}) collective-permute-start(bf16[2,128,128]{1,0,2:T(2,128)(2,1)S(1)} %slice.38), channel_id=1, source_target_pairs={{0,64},{16,80},{32,96},{48,112},{64,128},{80,144},{96,160},{112,17... | collective-permute-start | bytes 196616 | tf_op jit(solution)/shard_map/ppermute | solution.py:16
  51.3 13.7 %collective-permute-start.2 = (bf16[2,128,128]{1,0,2:T(2,128)(2,1)S(1)}, bf16[2,128,128]{1,0,2:T(2,128)(2,1)S(1)}, u32[]{:S(2)}, u32[]{:S(2)}) collective-permute-start(bf16[2,128,128]{1,0,2:T(2,128)(2,1)S(1)} %slice.38), channel_id=1, source_target_pairs={{0,48},{16,64},{32,80},{48,96},{64,112},{80,128},{96,144},{112,160... | collective-permute-start | bytes 196616 | tf_op jit(solution)/shard_map/ppermute | solution.py:16
  53.3 11.9 %collective-permute-start.3 = (bf16[2,128,128]{1,0,2:T(2,128)(2,1)S(1)}, bf16[2,128,128]{1,0,2:T(2,128)(2,1)S(1)}, u32[]{:S(2)}, u32[]{:S(2)}) collective-permute-start(bf16[2,128,128]{1,0,2:T(2,128)(2,1)S(1)} %slice.38), channel_id=1, source_target_pairs={{0,32},{16,48},{32,64},{48,80},{64,96},{80,112},{96,128},{112,144}... | collective-permute-start | bytes 196616 | tf_op jit(solution)/shard_map/ppermute | solution.py:16
  58.8 6.5 %collective-permute-start.4 = (bf16[2,128,128]{1,0,2:T(2,128)(2,1)S(1)}, bf16[2,128,128]{1,0,2:T(2,128)(2,1)S(1)}, u32[]{:S(2)}, u32[]{:S(2)}) collective-permute-start(bf16[2,128,128]{1,0,2:T(2,128)(2,1)S(1)} %slice.38), channel_id=1, source_target_pairs={{0,16},{16,32},{32,48},{48,64},{64,80},{80,96},{96,112},{112,128},... | collective-permute-start | bytes 196616 | tf_op jit(solution)/shard_map/ppermute | solution.py:16
  63.0 5.6 %collective-permute-start = (bf16[2,32,128]{1,0,2:T(2,128)(2,1)S(1)}, bf16[2,32,128]{1,0,2:T(2,128)(2,1)S(1)}, u32[]{:S(2)}, u32[]{:S(2)}) collective-permute-start(bf16[2,32,128]{1,0,2:T(2,128)(2,1)S(1)} %slice.36), channel_id=1, source_target_pairs={{0,16},{16,32},{32,48},{48,64},{64,80},{80,96},{96,112},{112,128},... | collective-permute-start | bytes 49160 | tf_op jit(solution)/shard_map/ppermute | solution.py:16
  115.9 0.6 copy-start
  206.4 68.4 %all-to-all-start = ((bf16[16,256,256]{2,1,0:T(8,128)(2,1)}), bf16[16,256,256]{2,1,0:T(8,128)(2,1)S(1)}, u32[]{:S(2)}, u32[]{:S(2)}) async-start(bf16[16,256,256]{2,1,0:T(8,128)(2,1)} %bitcast.42), calls=%async_computation | async-start | bytes 4194304 | tf_op jit(solution)/shard_map/all_to_all | solution.py:86
  216.4 90.1 %all-gather.5.cloned.1.call-start = ((), (), s32[]{:S(2)}) async-start(), calls=%async_computation.2 | async-start | bytes 2228224 | tf_op jit(solution)/shard_map/all_gather | solution.py:89
Sparse Core Ops, SparseCore 0:
  116.7 89.6 all-gather.2
Sparse Core Ops, SparseCore 1:
  219.0 87.5 all-gather.4
where the time goes:
time: 318 us
  waiting for transfers between devices  181 us (57%)
  blocking collectives  37.1 us (12%)
  starting transfers between devices  29.6 us (9%)
  matrix products  24.2 us (8%)
  other arithmetic  20.2 us (6%)
  between operations  15 us (5%)
  local copies, waits for them, and re-layouts  7.77 us (2%)
    all_gather x1, waiting for transfers between devices, body(): every_token = lax.all_gather(attention, 'tok', axis=0, tiled=True)  89.8 us
    all_to_all x1, waiting for transfers between devices, body(): lax.all_to_all(every_token, 'head', split_axis=0, concat_axis=1, tiled=True)  57.8 us
    all_gather x1, blocking collectives, body(): features = lax.all_gather(kv, 'head', axis=2, tiled=True)  37.1 us
    all_gather x1, waiting for transfers between devices, body(): lax.all_gather(w_out, 'head', axis=0, tiled=True)  29.3 us
    ppermute x5, starting transfers between devices, shifted(): return lax.ppermute(x, axis, pairs)  19.5 us
    reduce_sum x4, other arithmetic, attend_block(): denominator = jnp.sum(exponent, axis=(2, 3))  12.5 us
    dot_general x4, matrix products, attend_block(): jnp.dot(weights.reshape(-1, first_part.shape[1]), first_part[1], preferre...  12.1 us
    all_to_all x1, starting transfers between devices, body(): lax.all_to_all(every_token, 'head', split_axis=0, concat_axis=1, tiled=True)  10 us
  transfers between devices with their start and end apart: 8, of which 4 were waited for; matrix products, arithmetic and copies ran while one was open for 1% of the time, Pallas kernels for 0%

commit v1 on v0

v1 whole, which is shorter than its diff:
```python
import functools
import math

import jax
import jax.numpy as jnp
from jax import lax
from jax.experimental import pallas as pl
from jax.experimental.pallas import tpu as pltpu
from jax.sharding import Mesh, PartitionSpec as P

HD = 128
W1 = 512
W2 = 32
BLOCK = 128
STEP = 8
TOK = ("yh", "z", "core")
HEAD = ("yl", "x")
ALL = TOK + HEAD
SIZES = (2, 8, 2, 4, 4)
FAR = -1e30
BF16 = jnp.bfloat16
F32 = jnp.float32


def flat(yh, z, core, yl, x):
    return (((yh * 8 + z) * 2 + core) * 4 + yl) * 4 + x


def places():
    for yh in range(2):
        for z in range(8):
            for core in range(2):
                for yl in range(4):
                    for x in range(4):
                        yield yh, z, core, yl, x


def attention_pairs():
    return [
        (flat(yh, z, core, yl, x), flat(yl // 2, 2 * x + core, yl % 2, 2 * yh + z // 4, z % 4))
        for yh, z, core, yl, x in places()
    ]


def weight_pairs():
    return [
        (flat(yh, z, core, yl, x), flat(yl // 2, z, yl % 2, 2 * yh + core, x))
        for yh, z, core, yl, x in places()
    ]


def attend_kernel(where_ref, q_ref, kv_ref, out_ref, k1_ref, v1_ref, k2_ref, v2_ref, live_ref, q32_ref, acc_ref):
    block = where_ref[0]
    scale = 3.0 / math.sqrt(HD) * math.log2(math.e)

    def piece(k):
        return kv_ref[:, 8 * k : 8 * k + 8, :].astype(F32).reshape(HD, BLOCK)

    for k in range(5):
        k1_ref[:, BLOCK * k : BLOCK * (k + 1)] = piece(k).astype(BF16)
        v1_ref[BLOCK * k : BLOCK * (k + 1), 0:HD] = piece(5 + k).T.astype(BF16)
    v1_ref[:, HD : 2 * HD] = jnp.ones((5 * BLOCK, HD), BF16)
    first = block == 0
    own_k2 = piece(11).T
    k2_ref[W2:, :] = own_k2
    k2_ref[0:W2, :] = jnp.where(first, jnp.broadcast_to(own_k2[0:1, :], (W2, HD)), piece(10).T[BLOCK - W2 :, :])
    v2_ref[W2:, :] = piece(13).T
    v2_ref[0:W2, :] = jnp.where(first, 0.0, piece(12).T[BLOCK - W2 :, :])
    live_ref[W2:, :] = jnp.ones((BLOCK, HD), F32)
    live_ref[0:W2, :] = jnp.where(first, jnp.zeros((W2, HD), F32), 1.0)
    q32_ref[...] = q_ref[...].astype(F32)
    bias = [jnp.where(block - 4 + k < 0, FAR, 0.0) for k in range(4)]
    column = lax.broadcasted_iota(jnp.int32, (STEP, BLOCK), 1)
    row = lax.broadcasted_iota(jnp.int32, (STEP, BLOCK), 0)

    def step(index, carry):
        start = pl.multiple_of(index * STEP, STEP)
        newer = column > row + start
        newer_all = jnp.broadcast_to(newer[None], (W2, STEP, BLOCK)).reshape(W2 * STEP, BLOCK)
        tile_bias = [jnp.where(newer, bias[0], 0.0)] + [jnp.full((STEP, BLOCK), bias[k], F32) for k in (1, 2, 3)]
        for head in range(2):
            query = q32_ref[pl.ds(start, STEP), HD * head : HD * (head + 1)]
            rows = [query * k2_ref[pl.ds(start + W2 - back, STEP), :] for back in range(W2)]
            query_key = jnp.concatenate(rows, axis=0).astype(BF16)
            scores = jnp.dot(query_key, k1_ref[...], preferred_element_type=F32)
            tiles = [jnp.where(newer_all, scores[:, 0:BLOCK], scores[:, 4 * BLOCK :])]
            tiles += [scores[:, BLOCK * k : BLOCK * (k + 1)] for k in (1, 2, 3)]
            peak = None
            for k in range(4):
                top = jnp.max(tiles[k].reshape(W2, STEP, BLOCK), axis=0) + tile_bias[k]
                peak = top if peak is None else jnp.maximum(peak, top)
            peak = jnp.max(peak, axis=1, keepdims=True) * scale
            weights = []
            for k in range(4):
                offset = tile_bias[k] - peak
                grown = tiles[k].reshape(W2, STEP, BLOCK) * scale + offset[None]
                weights.append(jnp.exp2(grown).reshape(W2 * STEP, BLOCK))
            mixed = [jnp.where(newer_all, weights[0], 0.0)] + weights[1:] + [jnp.where(newer_all, 0.0, weights[0])]
            mixed = jnp.concatenate([m.astype(BF16) for m in mixed], axis=1)
            value = jnp.dot(mixed, v1_ref[...], preferred_element_type=F32)
            total = jnp.zeros((STEP, HD), F32)
            denominator = jnp.zeros((STEP, HD), F32)
            for back in range(W2):
                part = value[STEP * back : STEP * (back + 1), :]
                total += part[:, 0:HD] * v2_ref[pl.ds(start + W2 - back, STEP), :]
                denominator += part[:, HD:] * live_ref[pl.ds(start + W2 - back, STEP), :]
            acc_ref[pl.ds(start, STEP), HD * head : HD * (head + 1)] = total / denominator
        return carry

    lax.fori_loop(0, BLOCK // STEP, step, 0)
    out_ref[...] = acc_ref[...].astype(BF16)


def attend(block, queries, window):
    return pl.pallas_call(
        attend_kernel,
        out_shape=jax.ShapeDtypeStruct((BLOCK, 2 * HD), BF16),
        in_specs=[
            pl.BlockSpec(memory_space=pltpu.SMEM),
            pl.BlockSpec(memory_space=pltpu.VMEM),
            pl.BlockSpec(memory_space=pltpu.VMEM),
        ],
        out_specs=pl.BlockSpec(memory_space=pltpu.VMEM),
        scratch_shapes=[
            pltpu.VMEM((HD, 5 * BLOCK), BF16),
            pltpu.VMEM((5 * BLOCK, 2 * HD), BF16),
            pltpu.VMEM((W2 + BLOCK, HD), F32),
            pltpu.VMEM((W2 + BLOCK, HD), F32),
            pltpu.VMEM((W2 + BLOCK, HD), F32),
            pltpu.VMEM((BLOCK, 2 * HD), F32),
            pltpu.VMEM((BLOCK, 2 * HD), F32),
        ],
        cost_estimate=pl.CostEstimate(flops=6_000_000_000, bytes_accessed=1_000_000, transcendentals=4_200_000),
        name="attend",
    )(block, queries, window)


def project_kernel(core_ref, a_ref, w_ref, keep_ref, send_ref):
    core = core_ref[0]
    for half in range(2):
        for slot in range(2):
            block = 2 * half + (core if slot == 0 else 1 - core)
            total = jnp.zeros((256, 256), F32)
            for x in range(4):
                total += jnp.dot(a_ref[x], w_ref[block, x], preferred_element_type=F32)
            if slot == 0:
                keep_ref[half] = total
            else:
                send_ref[half] = total.astype(send_ref.dtype)


def project(core, attention, weights):
    return pl.pallas_call(
        project_kernel,
        out_shape=(jax.ShapeDtypeStruct((2, 256, 256), F32), jax.ShapeDtypeStruct((2, 256, 256), F32)),
        in_specs=[
            pl.BlockSpec(memory_space=pltpu.SMEM),
            pl.BlockSpec(memory_space=pltpu.VMEM),
            pl.BlockSpec(memory_space=pltpu.VMEM),
        ],
        out_specs=(pl.BlockSpec(memory_space=pltpu.VMEM), pl.BlockSpec(memory_space=pltpu.VMEM)),
        cost_estimate=pl.CostEstimate(flops=540_000_000, bytes_accessed=4_000_000, transcendentals=0),
        name="project",
    )(core, attention, weights)


def chip_shift(x, by):
    pairs = []
    for chip in range(16 - by):
        other = chip + by
        for core in range(2):
            pairs.append((2 * chip + core, 2 * other + core))
    return lax.ppermute(x, TOK, pairs)


def body(queries, kv, w_out):
    yh = lax.axis_index("yh")
    core = lax.axis_index("core")
    block = lax.axis_index(TOK).astype(jnp.int32)
    raw = jnp.transpose(kv, (0, 2, 1))
    swap = [(0, 1), (1, 0)]
    with jax.named_scope("kv_core"):
        other = lax.ppermute(raw, "core", swap)
    pair = jnp.where(core == 0, jnp.stack([raw, other]), jnp.stack([other, raw]))
    with jax.named_scope("kv_chip1"):
        near = chip_shift(pair, 1)
    with jax.named_scope("kv_chip2"):
        far = chip_shift(pair[:, 0:2], 2)
    firsts = jnp.concatenate([far, near[:, 0:2], pair[:, 0:2]], axis=0)
    seconds = jnp.concatenate([near[1:2, 2:4], pair[:, 2:4]], axis=0)
    firsts = lax.dynamic_slice_in_dim(firsts, core, 5, 0)
    seconds = lax.dynamic_slice_in_dim(seconds, core, 2, 0)
    window = jnp.concatenate(
        [firsts[:, 0].reshape(40, 128), firsts[:, 1].reshape(40, 128), seconds[:, 0].reshape(16, 128), seconds[:, 1].reshape(16, 128)],
        axis=0,
    )
    with jax.named_scope("kv_head"):
        window = lax.all_to_all(jnp.broadcast_to(window[None], (16,) + window.shape), HEAD, 0, 0)
    with jax.named_scope("w_move"):
        moved = lax.ppermute(w_out, ALL, weight_pairs())
    with jax.named_scope("w_head"):
        weights = lax.all_to_all(jnp.broadcast_to(moved[None], (16,) + moved.shape), HEAD, 0, 0)
    weights = weights.reshape(4, 4, 256, 256)
    attention = attend(block.reshape(1), queries, window)
    with jax.named_scope("att_move"):
        attention = lax.ppermute(attention, ALL, attention_pairs())
    with jax.named_scope("att_z"):
        attention = lax.all_to_all(jnp.broadcast_to(attention[None], (8,) + attention.shape), "z", 0, 0)
    keep, send = project(core.astype(jnp.int32).reshape(1), attention.reshape(4, 256, 256), weights)
    with jax.named_scope("out_core"):
        got = lax.ppermute(send, "core", swap)
    summed = keep + got
    leaving = lax.dynamic_index_in_dim(summed, 1 - yh, 0, keepdims=False).astype(BF16)
    with jax.named_scope("out_yh"):
        arrived = lax.ppermute(leaving, "yh", swap)
    staying = lax.dynamic_index_in_dim(summed, yh, 0, keepdims=False)
    return (staying + arrived.astype(F32)).astype(BF16)


def solution(mesh):
    fine = Mesh(mesh.devices.reshape(SIZES), ALL)
    return jax.shard_map(
        body,
        mesh=fine,
        in_specs=(P(TOK, HEAD), P(None, TOK, HEAD), P(HEAD, TOK)),
        out_specs=P(HEAD, TOK),
        check_vma=False,
    )
```

time: 318 us -> 173 us (0.54)
  the two profiles are of different devices: /device:TPU:126 before, /device:TPU:8 now
where the time goes in v1:
time: 173 us
  waiting for transfers between devices  56.4 us (33%)
  blocking collectives  56 us (32%)
  starting transfers between devices  34.9 us (20%)
  Pallas kernels  20 us (12%)
  local copies, waits for them, and re-layouts  2.67 us (2%)
  other arithmetic  2.63 us (2%)
    all_to_all x1, blocking collectives, body(): lax.all_to_all(jnp.broadcast_to(moved[None], (16,) + moved.shape), HEAD,...  56 us
    pallas_call x1, Pallas kernels, attend(): pl.pallas_call(attend_kernel, out_shape=jax.ShapeDtypeStruct((BLOCK, 2 *...  16.6 us
    ppermute x1, waiting for transfers between devices, body(): attention = lax.ppermute(attention, ALL, attention_pairs())  14 us
    all_to_all x1, waiting for transfers between devices, body(): lax.all_to_all(jnp.broadcast_to(window[None], (16,) + window.shape), HEAD...  12.7 us
    all_to_all x1, waiting for transfers between devices, body(): lax.all_to_all(jnp.broadcast_to(attention[None], (8,) + attention.shape),...  12.1 us
    ppermute x2, starting transfers between devices, chip_shift(): return lax.ppermute(x, TOK, pairs)  10.4 us
    ppermute x1, waiting for transfers between devices, body(): arrived = lax.ppermute(leaving, 'yh', swap)  8.85 us
    all_to_all x1, starting transfers between devices, body(): lax.all_to_all(jnp.broadcast_to(window[None], (16,) + window.shape), HEAD...  7.8 us
  transfers between devices with their start and end apart: 9, of which 8 were waited for; matrix products, arithmetic and copies ran while one was open for 0% of the time, Pallas kernels for 0%

profile of v1, /device:TPU:8, one launch (start us, length us, event | category | flops | bytes accessed | tf_op | source)
XLA Modules:
  0.0 172.9 jit_solution(4860963057790980710)
XLA Ops:
  0.0 1.9 %collective-permute-start = (bf16[4,8,128]{2,1,0:T(8,128)(2,1)}, bf16[4,8,128]{2,1,0:T(8,128)(2,1)S(1)}, u32[]{:S(2)}, u32[]{:S(2)}) collective-permute-start(bf16[4,8,128]{2,1,0:T(8,128)(2,1)} %bitcast.24), channel_id=1, source_target_pairs={{0,16},{16,0},{1,17},{17,1},{2,18},{18,2},{3,19},{19,3},{4,20},{20... | collective-permute-start | bytes 24584 | tf_op jit(solution)/shard_map/kv_core/ppermute | solution.py:183
  1.9 1.3 collective-permute-done
  3.3 0.8 maximum_select_fusion
  4.0 4.3 %collective-permute-start.2 = (bf16[2,4,8,128]{3,2,1,0:T(8,128)(2,1)S(1)}, bf16[2,4,8,128]{3,2,1,0:T(8,128)(2,1)S(1)}, u32[]{:S(2)}, u32[]{:S(2)}) collective-permute-start(bf16[2,4,8,128]{3,2,1,0:T(8,128)(2,1)S(1)} %maximum_select_fusion), channel_id=1, source_target_pairs={{0,32},{16,48},{32,64},{48,80},{64,96},{80,112},{96,128},{112,144}... | collective-permute-start | bytes 49160 | tf_op jit(solution)/shard_map/kv_chip1/ppermute | solution.py:173
  8.3 6.1 %collective-permute-start.1 = (bf16[2,2,8,128]{3,2,1,0:T(8,128)(2,1)S(1)}, bf16[2,2,8,128]{3,2,1,0:T(8,128)(2,1)S(1)}, u32[]{:S(2)}, u32[]{:S(2)}) collective-permute-start(bf16[2,2,8,128]{3,2,1,0:T(8,128)(2,1)S(1)} %get-tuple-element.11), channel_id=1, source_target_pairs={{0,64},{16,80},{32,96},{48,112},{64,128},{80,144},{96,160},{112,17... | collective-permute-start | bytes 24584 | tf_op jit(solution)/shard_map/kv_chip2/ppermute | solution.py:173
  14.4 0.0 collective-permute-done.2
  14.4 1.3 collective-permute-done.1
  15.9 0.8 broadcast_in_dim.6
  16.7 7.8 %all-to-all-start = ((bf16[16,112,128]{2,1,0:T(8,128)(2,1)}), bf16[16,112,128]{2,1,0:T(8,128)(2,1)S(1)}, u32[]{:S(2)}, u32[]{:S(2)}) async-start(bf16[16,112,128]{2,1,0:T(8,128)(2,1)} %broadcast_in_dim.6), calls=%async_computation | async-start | bytes 917504 | tf_op jit(solution)/shard_map/kv_head/all_to_all | solution.py:198
  24.5 12.7 %all-to-all-done.kv_ref = bf16[16,112,128]{2,1,0:T(8,128)(2,1)S(1)} async-done(((bf16[16,112,128]{2,1,0:T(8,128)(2,1)}), bf16[16,112,128]{2,1,0:T(8,128)(2,1)S(1)}, u32[]{:S(2)}, u32[]{:S(2)}) %all-to-all-start) | async-done | bytes 458784 | tf_op jit(solution)/shard_map/kv_head/all_to_all | solution.py:198
  37.2 0.0 copy-start.1
  37.2 0.8 copy-done.1
  38.0 0.0 copy-start.2
  38.0 16.6 %attend.1 = bf16[128,256]{1,0:T(8,128)(2,1)} custom-call(s32[1]{0:T(128)} %bitcast.1.where_ref, bf16[128,256]{1,0:T(8,128)(2,1)} %q_ref.1, bf16[16,112,128]{2,1,0:T(8,128)(2,1)} %copy-done.1), custom_call_target="tpu_custom_call" | custom-call | flops 6000000000 | bytes 1000000 | tf_op jit(solution)/shard_map/attend/pallas_call | solution.py:115
  54.5 1.9 %collective-permute-start.3 = (bf16[128,256]{1,0:T(8,128)(2,1)}, bf16[128,256]{1,0:T(8,128)(2,1)S(1)}, u32[]{:S(2)}, u32[]{:S(2)}) collective-permute-start(bf16[128,256]{1,0:T(8,128)(2,1)} %attend.1), channel_id=1, source_target_pairs={{0,0},{1,64},{2,128},{3,192},{4,16},{5,80},{6,144},{7,208},{8,256}... | collective-permute-start | bytes 196616 | tf_op jit(solution)/shard_map/att_move/ppermute | solution.py:206
  56.5 14.0 %collective-permute-done.3 = bf16[128,256]{1,0:T(8,128)(2,1)S(1)} collective-permute-done((bf16[128,256]{1,0:T(8,128)(2,1)}, bf16[128,256]{1,0:T(8,128)(2,1)S(1)}, u32[]{:S(2)}, u32[]{:S(2)}) %collective-permute-start.3) | collective-permute-done | bytes 65568 | tf_op jit(solution)/shard_map/att_move/ppermute | solution.py:206
  70.5 0.8 broadcast_in_dim.7
  71.3 3.5 %all-to-all-start.1 = ((bf16[8,128,256]{2,1,0:T(8,128)(2,1)}), bf16[8,128,256]{2,1,0:T(8,128)(2,1)S(1)}, u32[]{:S(2)}, u32[]{:S(2)}) async-start(bf16[8,128,256]{2,1,0:T(8,128)(2,1)} %broadcast_in_dim.7), calls=%async_computation.1 | async-start | bytes 1048576 | tf_op jit(solution)/shard_map/att_z/all_to_all | solution.py:208
  74.8 0.0 copy-done.2
  74.8 2.2 %collective-permute-start.4 = (bf16[256,256]{1,0:T(8,128)(2,1)S(1)}, bf16[256,256]{1,0:T(8,128)(2,1)S(1)}, u32[]{:S(2)}, u32[]{:S(2)}) collective-permute-start(bf16[256,256]{1,0:T(8,128)(2,1)S(1)} %copy-done.2), channel_id=1, source_target_pairs={{0,0},{1,1},{2,2},{3,3},{4,16},{5,17},{6,18},{7,19},{8,256},{9,257... | collective-permute-start | bytes 393224 | tf_op jit(solution)/shard_map/w_move/ppermute | solution.py:200
  77.0 4.1 %collective-permute-done.4 = bf16[256,256]{1,0:T(8,128)(2,1)S(1)} collective-permute-done((bf16[256,256]{1,0:T(8,128)(2,1)S(1)}, bf16[256,256]{1,0:T(8,128)(2,1)S(1)}, u32[]{:S(2)}, u32[]{:S(2)}) %collective-permute-start.4) | collective-permute-done | bytes 131104 | tf_op jit(solution)/shard_map/w_move/ppermute | solution.py:200
  81.1 12.1 %all-to-all-done.1 = bf16[8,128,256]{2,1,0:T(8,128)(2,1)S(1)} async-done(((bf16[8,128,256]{2,1,0:T(8,128)(2,1)}), bf16[8,128,256]{2,1,0:T(8,128)(2,1)S(1)}, u32[]{:S(2)}, u32[]{:S(2)}) %all-to-all-start.1) | async-done | bytes 524320 | tf_op jit(solution)/shard_map/att_z/all_to_all | solution.py:208
  93.2 0.0 copy-start
  93.2 0.2 broadcast_in_dim.8
  93.4 56.0 %all_to_all.15 = bf16[16,256,256]{2,1,0:T(8,128)(2,1)} all-to-all(bf16[16,256,256]{2,1,0:T(8,128)(2,1)S(1)} %broadcast_in_dim.8), channel_id=1, replica_groups=mesh['yh'=2,'z'=8,'core'=2,'yl'=4,'x'=4] {'yl','x'}, dimensions={0} | all-to-all | bytes 4194304 | tf_op jit(solution)/shard_map/w_head/all_to_all | solution.py:202
  149.4 0.0 copy-done
  149.4 3.4 %project.1 = (f32[2,256,256]{2,1,0:T(8,128)}, f32[2,256,256]{2,1,0:T(8,128)}) custom-call(s32[1]{0:T(128)} %bitcast.core_ref, bf16[4,256,256]{2,1,0:T(8,128)(2,1)} %bitcast.23, bf16[4,4,256,256]{3,2,1,0:T(8,128)(2,1)} %bitcast.22), custom_call_target="tpu_custom_call" | custom-call | flops 540000000 | bytes 4000000 | tf_op jit(solution)/shard_map/project/pallas_call | solution.py:153
  152.9 1.9 %collective-permute-start.5 = (f32[2,256,256]{2,1,0:T(8,128)}, f32[2,256,256]{2,1,0:T(8,128)S(1)}, u32[]{:S(2)}, u32[]{:S(2)}) collective-permute-start(f32[2,256,256]{2,1,0:T(8,128)} %get-tuple-element.8), channel_id=1, source_target_pairs={{0,16},{16,0},{1,17},{17,1},{2,18},{18,2},{3,19},{19,3},{4,20},{20... | collective-permute-start | bytes 1572872 | tf_op jit(solution)/shard_map/out_core/ppermute | solution.py:211
  154.8 2.1 %collective-permute-done.5 = f32[2,256,256]{2,1,0:T(8,128)S(1)} collective-permute-done((f32[2,256,256]{2,1,0:T(8,128)}, f32[2,256,256]{2,1,0:T(8,128)S(1)}, u32[]{:S(2)}, u32[]{:S(2)}) %collective-permute-start.5) | collective-permute-done | bytes 524320 | tf_op jit(solution)/shard_map/out_core/ppermute | solution.py:211
  156.9 1.1 add.30
  158.0 5.3 %collective-permute-start.6 = (bf16[256,256]{1,0:T(8,128)(2,1)S(1)}, bf16[256,256]{1,0:T(8,128)(2,1)S(1)}, u32[]{:S(2)}, u32[]{:S(2)}) collective-permute-start(bf16[256,256]{1,0:T(8,128)(2,1)S(1)} %fusion.1), channel_id=1, source_target_pairs={{0,256},{256,0},{1,257},{257,1},{2,258},{258,2},{3,259},{259,3},{4... | collective-permute-start | bytes 393224 | tf_op jit(solution)/shard_map/out_yh/ppermute | solution.py:215
  163.3 8.8 %collective-permute-done.6 = bf16[256,256]{1,0:T(8,128)(2,1)S(1)} collective-permute-done((bf16[256,256]{1,0:T(8,128)(2,1)S(1)}, bf16[256,256]{1,0:T(8,128)(2,1)S(1)}, u32[]{:S(2)}, u32[]{:S(2)}) %collective-permute-start.6) | collective-permute-done | bytes 131104 | tf_op jit(solution)/shard_map/out_yh/ppermute | solution.py:215
  172.2 0.7 fusion
  (9 shorter events, 0.1 us)
Async XLA Ops:
  0.0 3.3 %collective-permute-start = (bf16[4,8,128]{2,1,0:T(8,128)(2,1)}, bf16[4,8,128]{2,1,0:T(8,128)(2,1)S(1)}, u32[]{:S(2)}, u32[]{:S(2)}) collective-permute-start(bf16[4,8,128]{2,1,0:T(8,128)(2,1)} %bitcast.24), channel_id=1, source_target_pairs={{0,16},{16,0},{1,17},{17,1},{2,18},{18,2},{3,19},{19,3},{4,20},{20... | collective-permute-start | bytes 24584 | tf_op jit(solution)/shard_map/kv_core/ppermute | solution.py:183
  4.0 10.4 %collective-permute-start.2 = (bf16[2,4,8,128]{3,2,1,0:T(8,128)(2,1)S(1)}, bf16[2,4,8,128]{3,2,1,0:T(8,128)(2,1)S(1)}, u32[]{:S(2)}, u32[]{:S(2)}) collective-permute-start(bf16[2,4,8,128]{3,2,1,0:T(8,128)(2,1)S(1)} %maximum_select_fusion), channel_id=1, source_target_pairs={{0,32},{16,48},{32,64},{48,80},{64,96},{80,112},{96,128},{112,144}... | collective-permute-start | bytes 49160 | tf_op jit(solution)/shard_map/kv_chip1/ppermute | solution.py:173
  8.3 7.4 %collective-permute-start.1 = (bf16[2,2,8,128]{3,2,1,0:T(8,128)(2,1)S(1)}, bf16[2,2,8,128]{3,2,1,0:T(8,128)(2,1)S(1)}, u32[]{:S(2)}, u32[]{:S(2)}) collective-permute-start(bf16[2,2,8,128]{3,2,1,0:T(8,128)(2,1)S(1)} %get-tuple-element.11), channel_id=1, source_target_pairs={{0,64},{16,80},{32,96},{48,112},{64,128},{80,144},{96,160},{112,17... | collective-permute-start | bytes 24584 | tf_op jit(solution)/shard_map/kv_chip2/ppermute | solution.py:173
  16.7 20.5 %all-to-all-start = ((bf16[16,112,128]{2,1,0:T(8,128)(2,1)}), bf16[16,112,128]{2,1,0:T(8,128)(2,1)S(1)}, u32[]{:S(2)}, u32[]{:S(2)}) async-start(bf16[16,112,128]{2,1,0:T(8,128)(2,1)} %broadcast_in_dim.6), calls=%async_computation | async-start | bytes 917504 | tf_op jit(solution)/shard_map/kv_head/all_to_all | solution.py:198
  37.2 0.8 copy-start.1
  38.0 36.8 %copy-start.2 = (bf16[256,256]{1,0:T(8,128)(2,1)S(1)}, bf16[256,256]{1,0:T(8,128)(2,1)}, u32[]{:S(2)}) copy-start(bf16[256,256]{1,0:T(8,128)(2,1)} %param.5) | copy-start | bytes 393220
  54.5 15.9 %collective-permute-start.3 = (bf16[128,256]{1,0:T(8,128)(2,1)}, bf16[128,256]{1,0:T(8,128)(2,1)S(1)}, u32[]{:S(2)}, u32[]{:S(2)}) collective-permute-start(bf16[128,256]{1,0:T(8,128)(2,1)} %attend.1), channel_id=1, source_target_pairs={{0,0},{1,64},{2,128},{3,192},{4,16},{5,80},{6,144},{7,208},{8,256}... | collective-permute-start | bytes 196616 | tf_op jit(solution)/shard_map/att_move/ppermute | solution.py:206
  71.3 21.9 %all-to-all-start.1 = ((bf16[8,128,256]{2,1,0:T(8,128)(2,1)}), bf16[8,128,256]{2,1,0:T(8,128)(2,1)S(1)}, u32[]{:S(2)}, u32[]{:S(2)}) async-start(bf16[8,128,256]{2,1,0:T(8,128)(2,1)} %broadcast_in_dim.7), calls=%async_computation.1 | async-start | bytes 1048576 | tf_op jit(solution)/shard_map/att_z/all_to_all | solution.py:208
  74.8 6.3 %collective-permute-start.4 = (bf16[256,256]{1,0:T(8,128)(2,1)S(1)}, bf16[256,256]{1,0:T(8,128)(2,1)S(1)}, u32[]{:S(2)}, u32[]{:S(2)}) collective-permute-start(bf16[256,256]{1,0:T(8,128)(2,1)S(1)} %copy-done.2), channel_id=1, source_target_pairs={{0,0},{1,1},{2,2},{3,3},{4,16},{5,17},{6,18},{7,19},{8,256},{9,257... | collective-permute-start | bytes 393224 | tf_op jit(solution)/shard_map/w_move/ppermute | solution.py:200
  93.2 56.2 %copy-start = (bf16[8,128,256]{2,1,0:T(8,128)(2,1)}, bf16[8,128,256]{2,1,0:T(8,128)(2,1)S(1)}, u32[]{:S(2)}) copy-start(bf16[8,128,256]{2,1,0:T(8,128)(2,1)S(1)} %all-to-all-done.1) | copy-start | bytes 1572868
  152.9 4.0 %collective-permute-start.5 = (f32[2,256,256]{2,1,0:T(8,128)}, f32[2,256,256]{2,1,0:T(8,128)S(1)}, u32[]{:S(2)}, u32[]{:S(2)}) collective-permute-start(f32[2,256,256]{2,1,0:T(8,128)} %get-tuple-element.8), channel_id=1, source_target_pairs={{0,16},{16,0},{1,17},{17,1},{2,18},{18,2},{3,19},{19,3},{4,20},{20... | collective-permute-start | bytes 1572872 | tf_op jit(solution)/shard_map/out_core/ppermute | solution.py:211
  158.0 14.1 %collective-permute-start.6 = (bf16[256,256]{1,0:T(8,128)(2,1)S(1)}, bf16[256,256]{1,0:T(8,128)(2,1)S(1)}, u32[]{:S(2)}, u32[]{:S(2)}) collective-permute-start(bf16[256,256]{1,0:T(8,128)(2,1)S(1)} %fusion.1), channel_id=1, source_target_pairs={{0,256},{256,0},{1,257},{257,1},{2,258},{258,2},{3,259},{259,3},{4... | collective-permute-start | bytes 393224 | tf_op jit(solution)/shard_map/out_yh/ppermute | solution.py:215

commit v2 on v1

--- a/solution.py
+++ b/solution.py
@@ -1,4 +1,3 @@
-import functools
 import math
 
 import jax
@@ -8,8 +7,8 @@
 from jax.experimental.pallas import tpu as pltpu
 from jax.sharding import Mesh, PartitionSpec as P
 
+
 HD = 128
-W1 = 512
 W2 = 32
 BLOCK = 128
 STEP = 8
@@ -111,6 +110,32 @@
     out_ref[...] = acc_ref[...].astype(BF16)
 
 
+def window_kernel(parity_ref, all_ref, out_ref):
+    parity = parity_ref[0]
+    for column in range(16):
+        last = 2 * column + parity
+        for k in range(5):
+            source = jnp.maximum(last - 4 + k, 0)
+            out_ref[column, 8 * k : 8 * (k + 1), :] = all_ref[source, 0]
+            out_ref[column, 8 * (5 + k) : 8 * (6 + k), :] = all_ref[source, 1]
+        for k in range(2):
+            source = jnp.maximum(last - 1 + k, 0)
+            out_ref[column, 8 * (10 + k) : 8 * (11 + k), :] = all_ref[source, 2]
+            out_ref[column, 8 * (12 + k) : 8 * (13 + k), :] = all_ref[source, 3]
+
+
+def windows_of(parity, everything):
+    return pl.pallas_call(
+        window_kernel,
+        out_shape=jax.ShapeDtypeStruct((16, 112, 128), BF16),
+        in_specs=[pl.BlockSpec(memory_space=pltpu.SMEM), pl.BlockSpec(memory_space=pltpu.VMEM)],
+        out_specs=pl.BlockSpec(memory_space=pltpu.VMEM),
+        cost_estimate=pl.CostEstimate(flops=0, bytes_accessed=700_000, transcendentals=0),
+        compiler_params=pltpu.CompilerParams(vmem_limit_bytes=16 * 2**20),
+        name="windows",
+    )(parity, everything)
+
+
 def attend(block, queries, window):
     return pl.pallas_call(
         attend_kernel,
@@ -131,88 +156,68 @@
             pltpu.VMEM((BLOCK, 2 * HD), F32),
         ],
         cost_estimate=pl.CostEstimate(flops=6_000_000_000, bytes_accessed=1_000_000, transcendentals=4_200_000),
+        compiler_params=pltpu.CompilerParams(vmem_limit_bytes=16 * 2**20),
         name="attend",
     )(block, queries, window)
 
 
-def project_kernel(core_ref, a_ref, w_ref, keep_ref, send_ref):
-    core = core_ref[0]
+def project_kernel(place_ref, a_ref, w0_ref, w1_ref, w2_ref, w3_ref, keep_ref, send_ref):
+    core, yl, x = place_ref[0], place_ref[1], place_ref[2]
     for half in range(2):
         for slot in range(2):
-            block = 2 * half + (core if slot == 0 else 1 - core)
+            block = lax.bitwise_xor(2 * half + (core if slot == 0 else 1 - core), yl)
             total = jnp.zeros((256, 256), F32)
-            for x in range(4):
-                total += jnp.dot(a_ref[x], w_ref[block, x], preferred_element_type=F32)
+            for away, w_ref in enumerate((w0_ref, w1_ref, w2_ref, w3_ref)):
+                total += jnp.dot(a_ref[lax.bitwise_xor(x, away)], w_ref[block], preferred_element_type=F32)
             if slot == 0:
                 keep_ref[half] = total
             else:
-                send_ref[half] = total.astype(send_ref.dtype)
-
-
-def project(core, attention, weights):
+                send_ref[half] = total
+
+
+def project(place, attention, weights):
     return pl.pallas_call(
         project_kernel,
         out_shape=(jax.ShapeDtypeStruct((2, 256, 256), F32), jax.ShapeDtypeStruct((2, 256, 256), F32)),
-        in_specs=[
-            pl.BlockSpec(memory_space=pltpu.SMEM),
-            pl.BlockSpec(memory_space=pltpu.VMEM),
-            pl.BlockSpec(memory_space=pltpu.VMEM),
-        ],
+        in_specs=[pl.BlockSpec(memory_space=pltpu.SMEM)] + [pl.BlockSpec(memory_space=pltpu.VMEM)] * 5,
         out_specs=(pl.BlockSpec(memory_space=pltpu.VMEM), pl.BlockSpec(memory_space=pltpu.VMEM)),
         cost_estimate=pl.CostEstimate(flops=540_000_000, bytes_accessed=4_000_000, transcendentals=0),
+        compiler_params=pltpu.CompilerParams(vmem_limit_bytes=16 * 2**20),
         name="project",
-    )(core, attention, weights)
-
-
-def chip_shift(x, by):
-    pairs = []
-    for chip in range(16 - by):
-        other = chip + by
-        for core in range(2):
-            pairs.append((2 * chip + core, 2 * other + core))
-    return lax.ppermute(x, TOK, pairs)
-
-
-def body(queries, kv, w_out):
-    yh = lax.axis_index("yh")
-    core = lax.axis_index("core")
-    block = lax.axis_index(TOK).astype(jnp.int32)
+    )(place, attention, *weights)
+
+
+def across(x, axis, away):
+    count = lax.axis_size(axis)
+    return lax.ppermute(x, axis, [(i, i ^ away) for i in range(count)])
+
+
+def layer(queries, kv, w_out):
+    yh, z, core, yl, x = (lax.axis_index(name).astype(jnp.int32) for name in ALL)
+    parity = z % 2
+    block = 2 * (4 * yl + x) + parity
+    moved = lax.ppermute(w_out, ALL, weight_pairs())
+    queries = lax.ppermute(queries, ALL, attention_pairs())
     raw = jnp.transpose(kv, (0, 2, 1))
-    swap = [(0, 1), (1, 0)]
-    with jax.named_scope("kv_core"):
-        other = lax.ppermute(raw, "core", swap)
+    other = across(raw, "core", 1)
     pair = jnp.where(core == 0, jnp.stack([raw, other]), jnp.stack([other, raw]))
-    with jax.named_scope("kv_chip1"):
-        near = chip_shift(pair, 1)
-    with jax.named_scope("kv_chip2"):
-        far = chip_shift(pair[:, 0:2], 2)
-    firsts = jnp.concatenate([far, near[:, 0:2], pair[:, 0:2]], axis=0)
-    seconds = jnp.concatenate([near[1:2, 2:4], pair[:, 2:4]], axis=0)
-    firsts = lax.dynamic_slice_in_dim(firsts, core, 5, 0)
-    seconds = lax.dynamic_slice_in_dim(seconds, core, 2, 0)
-    window = jnp.concatenate(
-        [firsts[:, 0].reshape(40, 128), firsts[:, 1].reshape(40, 128), seconds[:, 0].reshape(16, 128), seconds[:, 1].reshape(16, 128)],
-        axis=0,
-    )
-    with jax.named_scope("kv_head"):
-        window = lax.all_to_all(jnp.broadcast_to(window[None], (16,) + window.shape), HEAD, 0, 0)
-    with jax.named_scope("w_move"):
-        moved = lax.ppermute(w_out, ALL, weight_pairs())
-    with jax.named_scope("w_head"):
-        weights = lax.all_to_all(jnp.broadcast_to(moved[None], (16,) + moved.shape), HEAD, 0, 0)
-    weights = weights.reshape(4, 4, 256, 256)
+    everything = lax.all_to_all(jnp.broadcast_to(pair[None], (16,) + pair.shape), ("yh", "z"), 0, 0)
+    columns = [moved]
+    for away in (1, 2, 3):
+        columns.append(across(moved, "yl", away))
+    columns = jnp.stack(columns)
+    weights = [columns]
+    for away in (1, 2, 3):
+        weights.append(across(columns, "x", away))
+    window = windows_of(parity.reshape(1), everything.reshape(32, 4, 8, 128))
+    window = lax.all_to_all(window, HEAD, 0, 0)
     attention = attend(block.reshape(1), queries, window)
-    with jax.named_scope("att_move"):
-        attention = lax.ppermute(attention, ALL, attention_pairs())
-    with jax.named_scope("att_z"):
-        attention = lax.all_to_all(jnp.broadcast_to(attention[None], (8,) + attention.shape), "z", 0, 0)
-    keep, send = project(core.astype(jnp.int32).reshape(1), attention.reshape(4, 256, 256), weights)
-    with jax.named_scope("out_core"):
-        got = lax.ppermute(send, "core", swap)
+    attention = lax.all_to_all(jnp.broadcast_to(attention[None], (8,) + attention.shape), "z", 0, 0)
+    keep, send = project(jnp.stack([core, yl, x]), attention.reshape(4, 256, 256), weights)
+    got = across(send, "core", 1)
     summed = keep + got
     leaving = lax.dynamic_index_in_dim(summed, 1 - yh, 0, keepdims=False).astype(BF16)
-    with jax.named_scope("out_yh"):
-        arrived = lax.ppermute(leaving, "yh", swap)
+    arrived = across(leaving, "yh", 1)
     staying = lax.dynamic_index_in_dim(summed, yh, 0, keepdims=False)
     return (staying + arrived.astype(F32)).astype(BF16)
 
@@ -220,7 +225,7 @@
 def solution(mesh):
     fine = Mesh(mesh.devices.reshape(SIZES), ALL)
     return jax.shard_map(
-        body,
+        layer,
         mesh=fine,
         in_specs=(P(TOK, HEAD), P(None, TOK, HEAD), P(HEAD, TOK)),
         out_specs=P(HEAD, TOK),

time: 173 us -> 162 us (0.936)
  the two profiles are of different devices: /device:TPU:8 before, /device:TPU:15 now
where the time goes in v2:
time: 162 us; the launch traced here: 161 us
  waiting for transfers between devices  73.4 us (45%)
  starting transfers between devices  67 us (41%)
  Pallas kernels  17.7 us (11%)
  local copies, waits for them, and re-layouts  1.62 us (1%)
    ppermute x9, waiting for transfers between devices, across(): return lax.ppermute(x, axis, [(i, i ^ away) for i in range(count)])  45.6 us
    ppermute x9, starting transfers between devices, across(): return lax.ppermute(x, axis, [(i, i ^ away) for i in range(count)])  39.3 us
    all_to_all x1, waiting for transfers between devices, layer(): lax.all_to_all(jnp.broadcast_to(pair[None], (16,) + pair.shape), ('yh', '...  15 us
    pallas_call x1, Pallas kernels, attend(): pl.pallas_call(attend_kernel, out_shape=jax.ShapeDtypeStruct((BLOCK, 2 *...  14.8 us
    all_to_all x1, starting transfers between devices, layer(): lax.all_to_all(jnp.broadcast_to(pair[None], (16,) + pair.shape), ('yh', '...  14.5 us
    ppermute x1, waiting for transfers between devices, layer(): queries = lax.ppermute(queries, ALL, attention_pairs())  12.8 us
    all_to_all x1, starting transfers between devices, layer(): window = lax.all_to_all(window, HEAD, 0, 0)  5.26 us
    ppermute x1, starting transfers between devices, layer(): queries = lax.ppermute(queries, ALL, attention_pairs())  3.65 us
  transfers between devices with their start and end apart: 14, of which 10 were waited for; matrix products, arithmetic and copies ran while one was open for 0% of the time, Pallas kernels for 0%

profile of v2, /device:TPU:15, one launch (start us, length us, event | category | flops | bytes accessed | tf_op | source)
XLA Modules:
  0.0 160.9 jit_solution(3205429638733395463)
XLA Ops:
  0.0 0.0 copy-start
  0.0 2.7 %collective-permute-start.1 = (bf16[4,8,128]{2,1,0:T(8,128)(2,1)}, bf16[4,8,128]{2,1,0:T(8,128)(2,1)S(1)}, u32[]{:S(2)}, u32[]{:S(2)}) collective-permute-start(bf16[4,8,128]{2,1,0:T(8,128)(2,1)} %bitcast.27), channel_id=1, source_target_pairs={{0,16},{16,0},{1,17},{17,1},{2,18},{18,2},{3,19},{19,3},{4,20},{20... | collective-permute-start | bytes 24584 | tf_op jit(solution)/shard_map/ppermute | solution.py:192
  2.7 1.0 collective-permute-done.1
  3.7 0.0 copy-done
  3.7 0.8 broadcast_in_dim.4
  4.5 14.5 %all-to-all-start = ((bf16[16,2,4,8,128]{4,3,2,1,0:T(8,128)(2,1)}), bf16[16,2,4,8,128]{4,3,2,1,0:T(8,128)(2,1)S(1)}, u32[]{:S(2)}, u32[]{:S(2)}) async-start(bf16[16,2,4,8,128]{4,3,2,1,0:T(8,128)(2,1)} %broadcast_in_dim.4), calls=%async_computation | async-start | bytes 524288 | tf_op jit(solution)/shard_map/all_to_all | solution.py:204
  19.0 15.0 %all-to-all-done = bf16[16,2,4,8,128]{4,3,2,1,0:T(8,128)(2,1)S(1)} async-done(((bf16[16,2,4,8,128]{4,3,2,1,0:T(8,128)(2,1)}), bf16[16,2,4,8,128]{4,3,2,1,0:T(8,128)(2,1)S(1)}, u32[]{:S(2)}, u32[]{:S(2)}) %all-to-all-start) | async-done | bytes 262176 | tf_op jit(solution)/shard_map/all_to_all | solution.py:204
  34.0 0.8 windows.1
  34.9 0.0 copy-start.2
  34.9 5.3 %all-to-all-start.1 = ((bf16[16,112,128]{2,1,0:T(8,128)(2,1)}), bf16[16,112,128]{2,1,0:T(8,128)(2,1)S(1)}, u32[]{:S(2)}, u32[]{:S(2)}) async-start(bf16[16,112,128]{2,1,0:T(8,128)(2,1)} %windows.1), calls=%async_computation.1 | async-start | bytes 917504 | tf_op jit(solution)/shard_map/all_to_all | solution.py:213
  40.1 0.0 copy-done.2
  40.1 3.6 %collective-permute-start = (bf16[128,256]{1,0:T(8,128)(2,1)S(1)}, bf16[128,256]{1,0:T(8,128)(2,1)S(1)}, u32[]{:S(2)}, u32[]{:S(2)}) collective-permute-start(bf16[128,256]{1,0:T(8,128)(2,1)S(1)} %copy-done.2), channel_id=1, source_target_pairs={{0,0},{1,64},{2,128},{3,192},{4,16},{5,80},{6,144},{7,208},{8,256}... | collective-permute-start | bytes 196616 | tf_op jit(solution)/shard_map/ppermute | solution.py:200
  43.8 12.8 %collective-permute-done.q_ref = bf16[128,256]{1,0:T(8,128)(2,1)S(1)} collective-permute-done((bf16[128,256]{1,0:T(8,128)(2,1)S(1)}, bf16[128,256]{1,0:T(8,128)(2,1)S(1)}, u32[]{:S(2)}, u32[]{:S(2)}) %collective-permute-start) | collective-permute-done | bytes 65568 | tf_op jit(solution)/shard_map/ppermute | solution.py:200
  56.6 0.0 all-to-all-done.1.kv_ref
  56.7 14.8 %attend.1 = bf16[128,256]{1,0:T(8,128)(2,1)S(1)} custom-call(s32[1]{0:T(128)} %bitcast.3.where_ref, bf16[128,256]{1,0:T(8,128)(2,1)S(1)} %collective-permute-done.q_ref, bf16[16,112,128]{2,1,0:T(8,128)(2,1)S(1)} %all-to-all-done.1.kv_ref), custom_call_target="tpu_custom_call" | custom-call | flops 6000000000 | bytes 1000000 | tf_op jit(solution)/shard_map/attend/pallas_call | solution.py:140
  71.5 0.8 broadcast_in_dim.5
  72.3 0.0 copy-start.1
  72.3 3.6 %all-to-all-start.2 = ((bf16[8,128,256]{2,1,0:T(8,128)(2,1)}), bf16[8,128,256]{2,1,0:T(8,128)(2,1)S(1)}, u32[]{:S(2)}, u32[]{:S(2)}) async-start(bf16[8,128,256]{2,1,0:T(8,128)(2,1)} %broadcast_in_dim.5), calls=%async_computation.2 | async-start | bytes 1048576 | tf_op jit(solution)/shard_map/all_to_all | solution.py:215
  75.9 0.0 copy-done.1
  75.9 0.7 collective-permute-start.2
  76.6 0.0 collective-permute-done.2
  76.6 5.6 %collective-permute-start.3 = (bf16[256,256]{1,0:T(8,128)(2,1)S(1)}, bf16[256,256]{1,0:T(8,128)(2,1)S(1)}, u32[]{:S(2)}, u32[]{:S(2)}) collective-permute-start(bf16[256,256]{1,0:T(8,128)(2,1)S(1)} %collective-permute-done.2), channel_id=1, source_target_pairs={{0,4},{4,0},{8,12},{12,8},{1,5},{5,1},{9,13},{13,9},{2,6},{6,2},{1... | collective-permute-start | bytes 393224 | tf_op jit(solution)/shard_map/ppermute | solution.py:192
  82.2 10.5 %collective-permute-start.4 = (bf16[256,256]{1,0:T(8,128)(2,1)S(1)}, bf16[256,256]{1,0:T(8,128)(2,1)S(1)}, u32[]{:S(2)}, u32[]{:S(2)}) collective-permute-start(bf16[256,256]{1,0:T(8,128)(2,1)S(1)} %collective-permute-done.2), channel_id=1, source_target_pairs={{0,8},{4,12},{8,0},{12,4},{1,9},{5,13},{9,1},{13,5},{2,10},{6,14},... | collective-permute-start | bytes 393224 | tf_op jit(solution)/shard_map/ppermute | solution.py:192
  92.7 1.9 %collective-permute-start.5 = (bf16[256,256]{1,0:T(8,128)(2,1)S(1)}, bf16[256,256]{1,0:T(8,128)(2,1)S(1)}, u32[]{:S(2)}, u32[]{:S(2)}) collective-permute-start(bf16[256,256]{1,0:T(8,128)(2,1)S(1)} %collective-permute-done.2), channel_id=1, source_target_pairs={{0,12},{4,8},{8,4},{12,0},{1,13},{5,9},{9,5},{13,1},{2,14},{6,10},... | collective-permute-start | bytes 393224 | tf_op jit(solution)/shard_map/ppermute | solution.py:192
  94.7 0.0 collective-permute-done.3
  94.7 1.1 collective-permute-done.4
  95.8 8.6 %collective-permute-done.5 = bf16[256,256]{1,0:T(8,128)(2,1)S(1)} collective-permute-done((bf16[256,256]{1,0:T(8,128)(2,1)S(1)}, bf16[256,256]{1,0:T(8,128)(2,1)S(1)}, u32[]{:S(2)}, u32[]{:S(2)}) %collective-permute-start.5) | collective-permute-done | bytes 131104 | tf_op jit(solution)/shard_map/ppermute | solution.py:192
  104.3 0.1 pad_maximum_fusion.w0_ref
  104.4 3.3 %collective-permute-start.6 = (bf16[4,256,256]{2,1,0:T(8,128)(2,1)S(1)}, bf16[4,256,256]{2,1,0:T(8,128)(2,1)S(1)}, u32[]{:S(2)}, u32[]{:S(2)}) collective-permute-start(bf16[4,256,256]{2,1,0:T(8,128)(2,1)S(1)} %pad_maximum_fusion.w0_ref), channel_id=1, source_target_pairs={{0,1},{1,0},{2,3},{3,2},{4,5},{5,4},{6,7},{7,6},{8,9},{9,8},{10,11... | collective-permute-start | bytes 1572872 | tf_op jit(solution)/shard_map/ppermute | solution.py:192
  107.7 4.5 %collective-permute-start.7 = (bf16[4,256,256]{2,1,0:T(8,128)(2,1)S(1)}, bf16[4,256,256]{2,1,0:T(8,128)(2,1)S(1)}, u32[]{:S(2)}, u32[]{:S(2)}) collective-permute-start(bf16[4,256,256]{2,1,0:T(8,128)(2,1)S(1)} %pad_maximum_fusion.w0_ref), channel_id=1, source_target_pairs={{0,2},{1,3},{2,0},{3,1},{4,6},{5,7},{6,4},{7,5},{8,10},{9,11},{10,... | collective-permute-start | bytes 1572872 | tf_op jit(solution)/shard_map/ppermute | solution.py:192
  112.2 1.9 %collective-permute-start.8 = (bf16[4,256,256]{2,1,0:T(8,128)(2,1)S(1)}, bf16[4,256,256]{2,1,0:T(8,128)(2,1)S(1)}, u32[]{:S(2)}, u32[]{:S(2)}) collective-permute-start(bf16[4,256,256]{2,1,0:T(8,128)(2,1)S(1)} %pad_maximum_fusion.w0_ref), channel_id=1, source_target_pairs={{0,3},{1,2},{2,1},{3,0},{4,7},{5,6},{6,5},{7,4},{8,11},{9,10},{10,... | collective-permute-start | bytes 1572872 | tf_op jit(solution)/shard_map/ppermute | solution.py:192
  114.1 0.1 pad_add_fusion.place_ref
  114.2 4.5 %collective-permute-done.6.w1_ref = bf16[4,256,256]{2,1,0:T(8,128)(2,1)S(1)} collective-permute-done((bf16[4,256,256]{2,1,0:T(8,128)(2,1)S(1)}, bf16[4,256,256]{2,1,0:T(8,128)(2,1)S(1)}, u32[]{:S(2)}, u32[]{:S(2)}) %collective-permute-start.6) | collective-permute-done | bytes 524320 | tf_op jit(solution)/shard_map/ppermute | solution.py:192
  118.7 14.0 %collective-permute-done.7.w2_ref = bf16[4,256,256]{2,1,0:T(8,128)(2,1)S(1)} collective-permute-done((bf16[4,256,256]{2,1,0:T(8,128)(2,1)S(1)}, bf16[4,256,256]{2,1,0:T(8,128)(2,1)S(1)}, u32[]{:S(2)}, u32[]{:S(2)}) %collective-permute-start.7) | collective-permute-done | bytes 524320 | tf_op jit(solution)/shard_map/ppermute | solution.py:192
  132.7 5.9 %collective-permute-done.8.w3_ref = bf16[4,256,256]{2,1,0:T(8,128)(2,1)S(1)} collective-permute-done((bf16[4,256,256]{2,1,0:T(8,128)(2,1)S(1)}, bf16[4,256,256]{2,1,0:T(8,128)(2,1)S(1)}, u32[]{:S(2)}, u32[]{:S(2)}) %collective-permute-start.8) | collective-permute-done | bytes 524320 | tf_op jit(solution)/shard_map/ppermute | solution.py:192
  138.6 0.0 all-to-all-done.2
  138.6 2.0 %project.1 = (f32[2,256,256]{2,1,0:T(8,128)S(1)}, f32[2,256,256]{2,1,0:T(8,128)}) custom-call(s32[3]{0:T(128)S(1)} %pad_add_fusion.place_ref, bf16[4,256,256]{2,1,0:T(8,128)(2,1)S(1)} %bitcast.21, bf16[4,256,256]{2,1,0:T(8,128)(2,1)S(1)} %pad_maximum_fusion.w0_ref, bf16[4,256,256]{2,1,0:T(8,128)(2,1)S(1)} %collective-permute-done.6.w1_ref, ...), custom_call_target="tpu_custom_call" | custom-call | flops 540000000 | bytes 4000000 | tf_op jit(solution)/shard_map/project/pallas_call | solution.py:179
  140.6 4.2 %collective-permute-start.9 = (f32[2,256,256]{2,1,0:T(8,128)}, f32[2,256,256]{2,1,0:T(8,128)S(1)}, u32[]{:S(2)}, u32[]{:S(2)}) collective-permute-start(f32[2,256,256]{2,1,0:T(8,128)} %get-tuple-element.8), channel_id=1, source_target_pairs={{0,16},{16,0},{1,17},{17,1},{2,18},{18,2},{3,19},{19,3},{4,20},{20... | collective-permute-start | bytes 1572872 | tf_op jit(solution)/shard_map/ppermute | solution.py:192
  144.8 1.7 %collective-permute-done.9 = f32[2,256,256]{2,1,0:T(8,128)S(1)} collective-permute-done((f32[2,256,256]{2,1,0:T(8,128)}, f32[2,256,256]{2,1,0:T(8,128)S(1)}, u32[]{:S(2)}, u32[]{:S(2)}) %collective-permute-start.9) | collective-permute-done | bytes 524320 | tf_op jit(solution)/shard_map/ppermute | solution.py:192
  146.5 0.1 add.27
  146.6 4.8 %collective-permute-start.10 = (bf16[256,256]{1,0:T(8,128)(2,1)S(1)}, bf16[256,256]{1,0:T(8,128)(2,1)S(1)}, u32[]{:S(2)}, u32[]{:S(2)}) collective-permute-start(bf16[256,256]{1,0:T(8,128)(2,1)S(1)} %fusion.1), channel_id=1, source_target_pairs={{0,256},{256,0},{1,257},{257,1},{2,258},{258,2},{3,259},{259,3},{4... | collective-permute-start | bytes 393224 | tf_op jit(solution)/shard_map/ppermute | solution.py:192
  151.4 8.8 %collective-permute-done.10 = bf16[256,256]{1,0:T(8,128)(2,1)S(1)} collective-permute-done((bf16[256,256]{1,0:T(8,128)(2,1)S(1)}, bf16[256,256]{1,0:T(8,128)(2,1)S(1)}, u32[]{:S(2)}, u32[]{:S(2)}) %collective-permute-start.10) | collective-permute-done | bytes 131104 | tf_op jit(solution)/shard_map/ppermute | solution.py:192
  160.2 0.7 fusion
  (2 shorter events, 0.0 us)
Async XLA Ops:
  0.0 3.7 %copy-start = (bf16[4,128,8]{1,2,0:T(8,128)(2,1)S(1)}, bf16[4,128,8]{1,2,0:T(8,128)(2,1)}, u32[]{:S(2)}) copy-start(bf16[4,128,8]{1,2,0:T(8,128)(2,1)} %param.4) | copy-start | bytes 24580
  0.0 3.7 %collective-permute-start.1 = (bf16[4,8,128]{2,1,0:T(8,128)(2,1)}, bf16[4,8,128]{2,1,0:T(8,128)(2,1)S(1)}, u32[]{:S(2)}, u32[]{:S(2)}) collective-permute-start(bf16[4,8,128]{2,1,0:T(8,128)(2,1)} %bitcast.27), channel_id=1, source_target_pairs={{0,16},{16,0},{1,17},{17,1},{2,18},{18,2},{3,19},{19,3},{4,20},{20... | collective-permute-start | bytes 24584 | tf_op jit(solution)/shard_map/ppermute | solution.py:192
  4.5 29.5 %all-to-all-start = ((bf16[16,2,4,8,128]{4,3,2,1,0:T(8,128)(2,1)}), bf16[16,2,4,8,128]{4,3,2,1,0:T(8,128)(2,1)S(1)}, u32[]{:S(2)}, u32[]{:S(2)}) async-start(bf16[16,2,4,8,128]{4,3,2,1,0:T(8,128)(2,1)} %broadcast_in_dim.4), calls=%async_computation | async-start | bytes 524288 | tf_op jit(solution)/shard_map/all_to_all | solution.py:204
  34.9 5.3 %copy-start.2 = (bf16[128,256]{1,0:T(8,128)(2,1)S(1)}, bf16[128,256]{1,0:T(8,128)(2,1)}, u32[]{:S(2)}) copy-start(bf16[128,256]{1,0:T(8,128)(2,1)} %param.3) | copy-start | bytes 196612
  34.9 21.8 %all-to-all-start.1 = ((bf16[16,112,128]{2,1,0:T(8,128)(2,1)}), bf16[16,112,128]{2,1,0:T(8,128)(2,1)S(1)}, u32[]{:S(2)}, u32[]{:S(2)}) async-start(bf16[16,112,128]{2,1,0:T(8,128)(2,1)} %windows.1), calls=%async_computation.1 | async-start | bytes 917504 | tf_op jit(solution)/shard_map/all_to_all | solution.py:213
  40.1 16.5 %collective-permute-start = (bf16[128,256]{1,0:T(8,128)(2,1)S(1)}, bf16[128,256]{1,0:T(8,128)(2,1)S(1)}, u32[]{:S(2)}, u32[]{:S(2)}) collective-permute-start(bf16[128,256]{1,0:T(8,128)(2,1)S(1)} %copy-done.2), channel_id=1, source_target_pairs={{0,0},{1,64},{2,128},{3,192},{4,16},{5,80},{6,144},{7,208},{8,256}... | collective-permute-start | bytes 196616 | tf_op jit(solution)/shard_map/ppermute | solution.py:200
  72.3 3.6 %copy-start.1 = (bf16[256,256]{1,0:T(8,128)(2,1)S(1)}, bf16[256,256]{1,0:T(8,128)(2,1)}, u32[]{:S(2)}) copy-start(bf16[256,256]{1,0:T(8,128)(2,1)} %param.5) | copy-start | bytes 393220
  72.3 66.3 %all-to-all-start.2 = ((bf16[8,128,256]{2,1,0:T(8,128)(2,1)}), bf16[8,128,256]{2,1,0:T(8,128)(2,1)S(1)}, u32[]{:S(2)}, u32[]{:S(2)}) async-start(bf16[8,128,256]{2,1,0:T(8,128)(2,1)} %broadcast_in_dim.5), calls=%async_computation.2 | async-start | bytes 1048576 | tf_op jit(solution)/shard_map/all_to_all | solution.py:215
  75.9 0.7 collective-permute-start.2
  76.6 18.0 %collective-permute-start.3 = (bf16[256,256]{1,0:T(8,128)(2,1)S(1)}, bf16[256,256]{1,0:T(8,128)(2,1)S(1)}, u32[]{:S(2)}, u32[]{:S(2)}) collective-permute-start(bf16[256,256]{1,0:T(8,128)(2,1)S(1)} %collective-permute-done.2), channel_id=1, source_target_pairs={{0,4},{4,0},{8,12},{12,8},{1,5},{5,1},{9,13},{13,9},{2,6},{6,2},{1... | collective-permute-start | bytes 393224 | tf_op jit(solution)/shard_map/ppermute | solution.py:192
  82.2 13.6 %collective-permute-start.4 = (bf16[256,256]{1,0:T(8,128)(2,1)S(1)}, bf16[256,256]{1,0:T(8,128)(2,1)S(1)}, u32[]{:S(2)}, u32[]{:S(2)}) collective-permute-start(bf16[256,256]{1,0:T(8,128)(2,1)S(1)} %collective-permute-done.2), channel_id=1, source_target_pairs={{0,8},{4,12},{8,0},{12,4},{1,9},{5,13},{9,1},{13,5},{2,10},{6,14},... | collective-permute-start | bytes 393224 | tf_op jit(solution)/shard_map/ppermute | solution.py:192
  92.7 11.6 %collective-permute-start.5 = (bf16[256,256]{1,0:T(8,128)(2,1)S(1)}, bf16[256,256]{1,0:T(8,128)(2,1)S(1)}, u32[]{:S(2)}, u32[]{:S(2)}) collective-permute-start(bf16[256,256]{1,0:T(8,128)(2,1)S(1)} %collective-permute-done.2), channel_id=1, source_target_pairs={{0,12},{4,8},{8,4},{12,0},{1,13},{5,9},{9,5},{13,1},{2,14},{6,10},... | collective-permute-start | bytes 393224 | tf_op jit(solution)/shard_map/ppermute | solution.py:192
  104.4 14.3 %collective-permute-start.6 = (bf16[4,256,256]{2,1,0:T(8,128)(2,1)S(1)}, bf16[4,256,256]{2,1,0:T(8,128)(2,1)S(1)}, u32[]{:S(2)}, u32[]{:S(2)}) collective-permute-start(bf16[4,256,256]{2,1,0:T(8,128)(2,1)S(1)} %pad_maximum_fusion.w0_ref), channel_id=1, source_target_pairs={{0,1},{1,0},{2,3},{3,2},{4,5},{5,4},{6,7},{7,6},{8,9},{9,8},{10,11... | collective-permute-start | bytes 1572872 | tf_op jit(solution)/shard_map/ppermute | solution.py:192
  107.7 25.0 %collective-permute-start.7 = (bf16[4,256,256]{2,1,0:T(8,128)(2,1)S(1)}, bf16[4,256,256]{2,1,0:T(8,128)(2,1)S(1)}, u32[]{:S(2)}, u32[]{:S(2)}) collective-permute-start(bf16[4,256,256]{2,1,0:T(8,128)(2,1)S(1)} %pad_maximum_fusion.w0_ref), channel_id=1, source_target_pairs={{0,2},{1,3},{2,0},{3,1},{4,6},{5,7},{6,4},{7,5},{8,10},{9,11},{10,... | collective-permute-start | bytes 1572872 | tf_op jit(solution)/shard_map/ppermute | solution.py:192
  112.2 26.4 %collective-permute-start.8 = (bf16[4,256,256]{2,1,0:T(8,128)(2,1)S(1)}, bf16[4,256,256]{2,1,0:T(8,128)(2,1)S(1)}, u32[]{:S(2)}, u32[]{:S(2)}) collective-permute-start(bf16[4,256,256]{2,1,0:T(8,128)(2,1)S(1)} %pad_maximum_fusion.w0_ref), channel_id=1, source_target_pairs={{0,3},{1,2},{2,1},{3,0},{4,7},{5,6},{6,5},{7,4},{8,11},{9,10},{10,... | collective-permute-start | bytes 1572872 | tf_op jit(solution)/shard_map/ppermute | solution.py:192
  140.6 5.9 %collective-permute-start.9 = (f32[2,256,256]{2,1,0:T(8,128)}, f32[2,256,256]{2,1,0:T(8,128)S(1)}, u32[]{:S(2)}, u32[]{:S(2)}) collective-permute-start(f32[2,256,256]{2,1,0:T(8,128)} %get-tuple-element.8), channel_id=1, source_target_pairs={{0,16},{16,0},{1,17},{17,1},{2,18},{18,2},{3,19},{19,3},{4,20},{20... | collective-permute-start | bytes 1572872 | tf_op jit(solution)/shard_map/ppermute | solution.py:192
  146.6 13.6 %collective-permute-start.10 = (bf16[256,256]{1,0:T(8,128)(2,1)S(1)}, bf16[256,256]{1,0:T(8,128)(2,1)S(1)}, u32[]{:S(2)}, u32[]{:S(2)}) collective-permute-start(bf16[256,256]{1,0:T(8,128)(2,1)S(1)} %fusion.1), channel_id=1, source_target_pairs={{0,256},{256,0},{1,257},{257,1},{2,258},{258,2},{3,259},{259,3},{4... | collective-permute-start | bytes 393224 | tf_op jit(solution)/shard_map/ppermute | solution.py:192

commit v3 on v2

--- a/solution.py
+++ b/solution.py
@@ -48,9 +48,12 @@
     ]
 
 
-def attend_kernel(where_ref, q_ref, kv_ref, out_ref, k1_ref, v1_ref, k2_ref, v2_ref, live_ref, q32_ref, acc_ref):
+def attend_kernel(
+    where_ref, q_ref, kv_ref, out_ref, k1_ref, v1_ref, k2_ref, v2_ref, live_ref, q32_ref, acc_ref, even_ref, odd_ref, tops_ref
+):
     block = where_ref[0]
     scale = 3.0 / math.sqrt(HD) * math.log2(math.e)
+    steps = BLOCK // STEP
 
     def piece(k):
         return kv_ref[:, 8 * k : 8 * k + 8, :].astype(F32).reshape(HD, BLOCK)
@@ -72,41 +75,63 @@
     column = lax.broadcasted_iota(jnp.int32, (STEP, BLOCK), 1)
     row = lax.broadcasted_iota(jnp.int32, (STEP, BLOCK), 0)
 
+    def newer_of(start):
+        newer = column > row + start
+        return newer, jnp.broadcast_to(newer[None], (W2, STEP, BLOCK)).reshape(W2 * STEP, BLOCK)
+
+    def produce(index, head, held_ref, top_ref):
+        start = pl.multiple_of(index * STEP, STEP)
+        _, newer_all = newer_of(start)
+        query = q32_ref[pl.ds(start, STEP), HD * head : HD * (head + 1)]
+        rows = [query * k2_ref[pl.ds(start + W2 - back, STEP), :] for back in range(W2)]
+        query_key = jnp.concatenate(rows, axis=0).astype(BF16)
+        scores = jnp.dot(query_key, k1_ref[...], preferred_element_type=F32)
+        held_ref[:, 0:BLOCK] = jnp.where(newer_all, scores[:, 0:BLOCK], scores[:, 4 * BLOCK :])
+        held_ref[:, BLOCK:] = scores[:, BLOCK : 4 * BLOCK]
+        newer, _ = newer_of(start)
+        tile_bias = [jnp.where(newer, bias[0], 0.0)] + [jnp.full((STEP, BLOCK), bias[k], F32) for k in (1, 2, 3)]
+        tiles = [jnp.where(newer_all, scores[:, 0:BLOCK], scores[:, 4 * BLOCK :])]
+        tiles += [scores[:, BLOCK * k : BLOCK * (k + 1)] for k in (1, 2, 3)]
+        peak = None
+        for k in range(4):
+            top = jnp.max(tiles[k].reshape(W2, STEP, BLOCK), axis=0) + tile_bias[k]
+            peak = top if peak is None else jnp.maximum(peak, top)
+        top_ref[...] = jnp.broadcast_to(jnp.max(peak, axis=1, keepdims=True) * scale, (STEP, BLOCK))
+
+    def consume(index, head, held_ref, top_ref):
+        start = pl.multiple_of(index * STEP, STEP)
+        newer, newer_all = newer_of(start)
+        tile_bias = [jnp.where(newer, bias[0], 0.0)] + [jnp.full((STEP, BLOCK), bias[k], F32) for k in (1, 2, 3)]
+        peak = top_ref[...]
+        weights = []
+        for k in range(4):
+            tile = held_ref[:, BLOCK * k : BLOCK * (k + 1)].reshape(W2, STEP, BLOCK)
+            grown = tile * scale + (tile_bias[k] - peak)[None]
+            weights.append(jnp.exp2(grown).reshape(W2 * STEP, BLOCK))
+        mixed = [jnp.where(newer_all, weights[0], 0.0)] + weights[1:] + [jnp.where(newer_all, 0.0, weights[0])]
+        mixed = jnp.concatenate([m.astype(BF16) for m in mixed], axis=1)
+        value = jnp.dot(mixed, v1_ref[...], preferred_element_type=F32)
+        total = jnp.zeros((STEP, HD), F32)
+        denominator = jnp.zeros((STEP, HD), F32)
+        for back in range(W2):
+            part = value[STEP * back : STEP * (back + 1), :]
+            total += part[:, 0:HD] * v2_ref[pl.ds(start + W2 - back, STEP), :]
+            denominator += part[:, HD:] * live_ref[pl.ds(start + W2 - back, STEP), :]
+        acc_ref[pl.ds(start, STEP), HD * head : HD * (head + 1)] = total / denominator
+
+    for head in range(2):
+        produce(0, head, even_ref.at[head], tops_ref.at[head])
+
     def step(index, carry):
-        start = pl.multiple_of(index * STEP, STEP)
-        newer = column > row + start
-        newer_all = jnp.broadcast_to(newer[None], (W2, STEP, BLOCK)).reshape(W2 * STEP, BLOCK)
-        tile_bias = [jnp.where(newer, bias[0], 0.0)] + [jnp.full((STEP, BLOCK), bias[k], F32) for k in (1, 2, 3)]
         for head in range(2):
-            query = q32_ref[pl.ds(start, STEP), HD * head : HD * (head + 1)]
-            rows = [query * k2_ref[pl.ds(start + W2 - back, STEP), :] for back in range(W2)]
-            query_key = jnp.concatenate(rows, axis=0).astype(BF16)
-            scores = jnp.dot(query_key, k1_ref[...], preferred_element_type=F32)
-            tiles = [jnp.where(newer_all, scores[:, 0:BLOCK], scores[:, 4 * BLOCK :])]
-            tiles += [scores[:, BLOCK * k : BLOCK * (k + 1)] for k in (1, 2, 3)]
-            peak = None
-            for k in range(4):
-                top = jnp.max(tiles[k].reshape(W2, STEP, BLOCK), axis=0) + tile_bias[k]
-                peak = top if peak is None else jnp.maximum(peak, top)
-            peak = jnp.max(peak, axis=1, keepdims=True) * scale
-            weights = []
-            for k in range(4):
-                offset = tile_bias[k] - peak
-                grown = tiles[k].reshape(W2, STEP, BLOCK) * scale + offset[None]
-                weights.append(jnp.exp2(grown).reshape(W2 * STEP, BLOCK))
-            mixed = [jnp.where(newer_all, weights[0], 0.0)] + weights[1:] + [jnp.where(newer_all, 0.0, weights[0])]
-            mixed = jnp.concatenate([m.astype(BF16) for m in mixed], axis=1)
-            value = jnp.dot(mixed, v1_ref[...], preferred_element_type=F32)
-            total = jnp.zeros((STEP, HD), F32)
-            denominator = jnp.zeros((STEP, HD), F32)
-            for back in range(W2):
-                part = value[STEP * back : STEP * (back + 1), :]
-                total += part[:, 0:HD] * v2_ref[pl.ds(start + W2 - back, STEP), :]
-                denominator += part[:, HD:] * live_ref[pl.ds(start + W2 - back, STEP), :]
-            acc_ref[pl.ds(start, STEP), HD * head : HD * (head + 1)] = total / denominator
+            produce(2 * index + 1, head, odd_ref.at[head], tops_ref.at[2 + head])
+            consume(2 * index, head, even_ref.at[head], tops_ref.at[head])
+        for head in range(2):
+            produce(jnp.minimum(2 * index + 2, steps - 1), head, even_ref.at[head], tops_ref.at[head])
+            consume(2 * index + 1, head, odd_ref.at[head], tops_ref.at[2 + head])
         return carry
 
-    lax.fori_loop(0, BLOCK // STEP, step, 0)
+    lax.fori_loop(0, steps // 2, step, 0)
     out_ref[...] = acc_ref[...].astype(BF16)
 
 
@@ -154,6 +179,9 @@
             pltpu.VMEM((W2 + BLOCK, HD), F32),
             pltpu.VMEM((BLOCK, 2 * HD), F32),
             pltpu.VMEM((BLOCK, 2 * HD), F32),
+            pltpu.VMEM((2, W2 * STEP, 4 * BLOCK), F32),
+            pltpu.VMEM((2, W2 * STEP, 4 * BLOCK), F32),
+            pltpu.VMEM((4, STEP, BLOCK), F32),
         ],
         cost_estimate=pl.CostEstimate(flops=6_000_000_000, bytes_accessed=1_000_000, transcendentals=4_200_000),
         compiler_params=pltpu.CompilerParams(vmem_limit_bytes=16 * 2**20),
@@ -202,10 +230,8 @@
     other = across(raw, "core", 1)
     pair = jnp.where(core == 0, jnp.stack([raw, other]), jnp.stack([other, raw]))
     everything = lax.all_to_all(jnp.broadcast_to(pair[None], (16,) + pair.shape), ("yh", "z"), 0, 0)
-    columns = [moved]
-    for away in (1, 2, 3):
-        columns.append(across(moved, "yl", away))
-    columns = jnp.stack(columns)
+    columns = jnp.stack([moved, across(moved, "yl", 1)])
+    columns = jnp.concatenate([columns, across(columns, "yl", 2)])
     weights = [columns]
     for away in (1, 2, 3):
         weights.append(across(columns, "x", away))

time: 162 us -> 147 us (0.907)
  the two profiles are of different devices: /device:TPU:15 before, /device:TPU:6 now
where the time goes in v3:
time: 147 us; the launch traced here: 146 us
  starting transfers between devices  77.1 us (52%)
  waiting for transfers between devices  54 us (37%)
  Pallas kernels  12.5 us (9%)
  local copies, waits for them, and re-layouts  1.61 us (1%)
    ppermute x8, starting transfers between devices, across(): return lax.ppermute(x, axis, [(i, i ^ away) for i in range(count)])  41.1 us
    ppermute x8, waiting for transfers between devices, across(): return lax.ppermute(x, axis, [(i, i ^ away) for i in range(count)])  41 us
    all_to_all x1, starting transfers between devices, layer(): lax.all_to_all(jnp.broadcast_to(pair[None], (16,) + pair.shape), ('yh', '...  15.7 us
    all_to_all x1, waiting for transfers between devices, layer(): lax.all_to_all(jnp.broadcast_to(pair[None], (16,) + pair.shape), ('yh', '...  13 us
    pallas_call x1, Pallas kernels, attend(): pl.pallas_call(attend_kernel, out_shape=jax.ShapeDtypeStruct((BLOCK, 2 *...  9.62 us
    all_to_all x1, starting transfers between devices, layer(): lax.all_to_all(jnp.broadcast_to(attention[None], (8,) + attention.shape),...  8.21 us
    all_to_all x1, starting transfers between devices, layer(): window = lax.all_to_all(window, HEAD, 0, 0)  7.63 us
    ppermute x1, starting transfers between devices, layer(): queries = lax.ppermute(queries, ALL, attention_pairs())  3.83 us
  transfers between devices with their start and end apart: 13, of which 8 were waited for; matrix products, arithmetic and copies ran while one was open for 1% of the time, Pallas kernels for 7%

profile of v3, /device:TPU:6, one launch (start us, length us, event | category | flops | bytes accessed | tf_op | source)
XLA Modules:
  0.0 146.4 jit_solution(12305885774225474950)
XLA Ops:
  0.0 0.0 copy-start
  0.0 2.0 %collective-permute-start.1 = (bf16[4,8,128]{2,1,0:T(8,128)(2,1)}, bf16[4,8,128]{2,1,0:T(8,128)(2,1)S(1)}, u32[]{:S(2)}, u32[]{:S(2)}) collective-permute-start(bf16[4,8,128]{2,1,0:T(8,128)(2,1)} %bitcast.25), channel_id=1, source_target_pairs={{0,16},{16,0},{1,17},{17,1},{2,18},{18,2},{3,19},{19,3},{4,20},{20... | collective-permute-start | bytes 24584 | tf_op jit(solution)/shard_map/ppermute | solution.py:220
  2.1 1.3 collective-permute-done.1
  3.4 0.0 copy-done
  3.4 0.7 broadcast_in_dim.4
  4.2 15.7 %all-to-all-start = ((bf16[16,2,4,8,128]{4,3,2,1,0:T(8,128)(2,1)}), bf16[16,2,4,8,128]{4,3,2,1,0:T(8,128)(2,1)S(1)}, u32[]{:S(2)}, u32[]{:S(2)}) async-start(bf16[16,2,4,8,128]{4,3,2,1,0:T(8,128)(2,1)} %broadcast_in_dim.4), calls=%async_computation | async-start | bytes 524288 | tf_op jit(solution)/shard_map/all_to_all | solution.py:232
  19.9 13.0 %all-to-all-done = bf16[16,2,4,8,128]{4,3,2,1,0:T(8,128)(2,1)S(1)} async-done(((bf16[16,2,4,8,128]{4,3,2,1,0:T(8,128)(2,1)}), bf16[16,2,4,8,128]{4,3,2,1,0:T(8,128)(2,1)S(1)}, u32[]{:S(2)}, u32[]{:S(2)}) %all-to-all-start) | async-done | bytes 262176 | tf_op jit(solution)/shard_map/all_to_all | solution.py:232
  32.9 0.8 windows.1
  33.7 0.0 copy-start.1
  33.7 0.0 copy-start.2
  33.7 7.6 %all-to-all-start.1 = ((bf16[16,112,128]{2,1,0:T(8,128)(2,1)}), bf16[16,112,128]{2,1,0:T(8,128)(2,1)S(1)}, u32[]{:S(2)}, u32[]{:S(2)}) async-start(bf16[16,112,128]{2,1,0:T(8,128)(2,1)} %windows.1), calls=%async_computation.1 | async-start | bytes 917504 | tf_op jit(solution)/shard_map/all_to_all | solution.py:239
  41.3 0.0 copy-done.1
  41.3 0.7 collective-permute-start.2
  42.0 0.0 copy-done.2
  42.0 3.8 %collective-permute-start = (bf16[128,256]{1,0:T(8,128)(2,1)S(1)}, bf16[128,256]{1,0:T(8,128)(2,1)S(1)}, u32[]{:S(2)}, u32[]{:S(2)}) collective-permute-start(bf16[128,256]{1,0:T(8,128)(2,1)S(1)} %copy-done.2), channel_id=1, source_target_pairs={{0,0},{1,64},{2,128},{3,192},{4,16},{5,80},{6,144},{7,208},{8,256}... | collective-permute-start | bytes 196616 | tf_op jit(solution)/shard_map/ppermute | solution.py:228
  45.9 0.0 collective-permute-done.2
  45.9 7.5 %collective-permute-start.3 = (bf16[256,256]{1,0:T(8,128)(2,1)S(1)}, bf16[256,256]{1,0:T(8,128)(2,1)S(1)}, u32[]{:S(2)}, u32[]{:S(2)}) collective-permute-start(bf16[256,256]{1,0:T(8,128)(2,1)S(1)} %collective-permute-done.2), channel_id=1, source_target_pairs={{0,4},{4,0},{8,12},{12,8},{1,5},{5,1},{9,13},{13,9},{2,6},{6,2},{1... | collective-permute-start | bytes 393224 | tf_op jit(solution)/shard_map/ppermute | solution.py:220
  53.4 0.0 collective-permute-done.q_ref
  53.4 0.0 all-to-all-done.1.kv_ref
  53.4 9.6 %attend.1 = bf16[128,256]{1,0:T(8,128)(2,1)S(1)} custom-call(s32[1]{0:T(128)} %bitcast.3.where_ref, bf16[128,256]{1,0:T(8,128)(2,1)S(1)} %collective-permute-done.q_ref, bf16[16,112,128]{2,1,0:T(8,128)(2,1)S(1)} %all-to-all-done.1.kv_ref), custom_call_target="tpu_custom_call" | custom-call | flops 6000000000 | bytes 1000000 | tf_op jit(solution)/shard_map/attend/pallas_call | solution.py:165
  63.1 0.8 broadcast_in_dim.5
  63.9 8.2 %all-to-all-start.2 = ((bf16[8,128,256]{2,1,0:T(8,128)(2,1)}), bf16[8,128,256]{2,1,0:T(8,128)(2,1)S(1)}, u32[]{:S(2)}, u32[]{:S(2)}) async-start(bf16[8,128,256]{2,1,0:T(8,128)(2,1)} %broadcast_in_dim.5), calls=%async_computation.2 | async-start | bytes 1048576 | tf_op jit(solution)/shard_map/all_to_all | solution.py:241
  72.1 0.0 collective-permute-done.3
  72.1 7.6 %collective-permute-start.4 = (bf16[2,256,256]{2,1,0:T(8,128)(2,1)S(1)}, bf16[2,256,256]{2,1,0:T(8,128)(2,1)S(1)}, u32[]{:S(2)}, u32[]{:S(2)}) collective-permute-start(bf16[2,256,256]{2,1,0:T(8,128)(2,1)S(1)} %pad_maximum_fusion.1), channel_id=1, source_target_pairs={{0,8},{4,12},{8,0},{12,4},{1,9},{5,13},{9,1},{13,5},{2,10},{6,14},... | collective-permute-start | bytes 786440 | tf_op jit(solution)/shard_map/ppermute | solution.py:220
  79.8 9.1 %collective-permute-done.4 = bf16[2,256,256]{2,1,0:T(8,128)(2,1)S(1)} collective-permute-done((bf16[2,256,256]{2,1,0:T(8,128)(2,1)S(1)}, bf16[2,256,256]{2,1,0:T(8,128)(2,1)S(1)}, u32[]{:S(2)}, u32[]{:S(2)}) %collective-permute-start.4) | collective-permute-done | bytes 262176 | tf_op jit(solution)/shard_map/ppermute | solution.py:220
  88.9 0.1 pad_maximum_fusion.w0_ref
  88.9 2.3 %collective-permute-start.5 = (bf16[4,256,256]{2,1,0:T(8,128)(2,1)S(1)}, bf16[4,256,256]{2,1,0:T(8,128)(2,1)S(1)}, u32[]{:S(2)}, u32[]{:S(2)}) collective-permute-start(bf16[4,256,256]{2,1,0:T(8,128)(2,1)S(1)} %pad_maximum_fusion.w0_ref), channel_id=1, source_target_pairs={{0,1},{1,0},{2,3},{3,2},{4,5},{5,4},{6,7},{7,6},{8,9},{9,8},{10,11... | collective-permute-start | bytes 1572872 | tf_op jit(solution)/shard_map/ppermute | solution.py:220
  91.3 3.8 %collective-permute-start.6 = (bf16[4,256,256]{2,1,0:T(8,128)(2,1)S(1)}, bf16[4,256,256]{2,1,0:T(8,128)(2,1)S(1)}, u32[]{:S(2)}, u32[]{:S(2)}) collective-permute-start(bf16[4,256,256]{2,1,0:T(8,128)(2,1)S(1)} %pad_maximum_fusion.w0_ref), channel_id=1, source_target_pairs={{0,2},{1,3},{2,0},{3,1},{4,6},{5,7},{6,4},{7,5},{8,10},{9,11},{10,... | collective-permute-start | bytes 1572872 | tf_op jit(solution)/shard_map/ppermute | solution.py:220
  95.1 4.3 %collective-permute-start.7 = (bf16[4,256,256]{2,1,0:T(8,128)(2,1)S(1)}, bf16[4,256,256]{2,1,0:T(8,128)(2,1)S(1)}, u32[]{:S(2)}, u32[]{:S(2)}) collective-permute-start(bf16[4,256,256]{2,1,0:T(8,128)(2,1)S(1)} %pad_maximum_fusion.w0_ref), channel_id=1, source_target_pairs={{0,3},{1,2},{2,1},{3,0},{4,7},{5,6},{6,5},{7,4},{8,11},{9,10},{10,... | collective-permute-start | bytes 1572872 | tf_op jit(solution)/shard_map/ppermute | solution.py:220
  99.4 0.1 pad_add_fusion.place_ref
  99.5 6.2 %collective-permute-done.5.w1_ref = bf16[4,256,256]{2,1,0:T(8,128)(2,1)S(1)} collective-permute-done((bf16[4,256,256]{2,1,0:T(8,128)(2,1)S(1)}, bf16[4,256,256]{2,1,0:T(8,128)(2,1)S(1)}, u32[]{:S(2)}, u32[]{:S(2)}) %collective-permute-start.5) | collective-permute-done | bytes 524320 | tf_op jit(solution)/shard_map/ppermute | solution.py:220
  105.6 9.0 %collective-permute-done.6.w2_ref = bf16[4,256,256]{2,1,0:T(8,128)(2,1)S(1)} collective-permute-done((bf16[4,256,256]{2,1,0:T(8,128)(2,1)S(1)}, bf16[4,256,256]{2,1,0:T(8,128)(2,1)S(1)}, u32[]{:S(2)}, u32[]{:S(2)}) %collective-permute-start.6) | collective-permute-done | bytes 524320 | tf_op jit(solution)/shard_map/ppermute | solution.py:220
  114.6 6.8 %collective-permute-done.7.w3_ref = bf16[4,256,256]{2,1,0:T(8,128)(2,1)S(1)} collective-permute-done((bf16[4,256,256]{2,1,0:T(8,128)(2,1)S(1)}, bf16[4,256,256]{2,1,0:T(8,128)(2,1)S(1)}, u32[]{:S(2)}, u32[]{:S(2)}) %collective-permute-start.7) | collective-permute-done | bytes 524320 | tf_op jit(solution)/shard_map/ppermute | solution.py:220
  121.4 0.0 all-to-all-done.2
  121.4 2.1 %project.1 = (f32[2,256,256]{2,1,0:T(8,128)S(1)}, f32[2,256,256]{2,1,0:T(8,128)}) custom-call(s32[3]{0:T(128)S(1)} %pad_add_fusion.place_ref, bf16[4,256,256]{2,1,0:T(8,128)(2,1)S(1)} %bitcast.19, bf16[4,256,256]{2,1,0:T(8,128)(2,1)S(1)} %pad_maximum_fusion.w0_ref, bf16[4,256,256]{2,1,0:T(8,128)(2,1)S(1)} %collective-permute-done.5.w1_ref, ...), custom_call_target="tpu_custom_call" | custom-call | flops 540000000 | bytes 4000000 | tf_op jit(solution)/shard_map/project/pallas_call | solution.py:207
  123.4 1.9 %collective-permute-start.8 = (f32[2,256,256]{2,1,0:T(8,128)}, f32[2,256,256]{2,1,0:T(8,128)S(1)}, u32[]{:S(2)}, u32[]{:S(2)}) collective-permute-start(f32[2,256,256]{2,1,0:T(8,128)} %get-tuple-element.8), channel_id=1, source_target_pairs={{0,16},{16,0},{1,17},{17,1},{2,18},{18,2},{3,19},{19,3},{4,20},{20... | collective-permute-start | bytes 1572872 | tf_op jit(solution)/shard_map/ppermute | solution.py:220
  125.4 2.1 %collective-permute-done.8 = f32[2,256,256]{2,1,0:T(8,128)S(1)} collective-permute-done((f32[2,256,256]{2,1,0:T(8,128)}, f32[2,256,256]{2,1,0:T(8,128)S(1)}, u32[]{:S(2)}, u32[]{:S(2)}) %collective-permute-start.8) | collective-permute-done | bytes 524320 | tf_op jit(solution)/shard_map/ppermute | solution.py:220
  127.4 0.1 add.27
  127.5 11.6 %collective-permute-start.9 = (bf16[256,256]{1,0:T(8,128)(2,1)S(1)}, bf16[256,256]{1,0:T(8,128)(2,1)S(1)}, u32[]{:S(2)}, u32[]{:S(2)}) collective-permute-start(bf16[256,256]{1,0:T(8,128)(2,1)S(1)} %fusion.1), channel_id=1, source_target_pairs={{0,256},{256,0},{1,257},{257,1},{2,258},{258,2},{3,259},{259,3},{4... | collective-permute-start | bytes 393224 | tf_op jit(solution)/shard_map/ppermute | solution.py:220
  139.1 6.6 %collective-permute-done.9 = bf16[256,256]{1,0:T(8,128)(2,1)S(1)} collective-permute-done((bf16[256,256]{1,0:T(8,128)(2,1)S(1)}, bf16[256,256]{1,0:T(8,128)(2,1)S(1)}, u32[]{:S(2)}, u32[]{:S(2)}) %collective-permute-start.9) | collective-permute-done | bytes 131104 | tf_op jit(solution)/shard_map/ppermute | solution.py:220
  145.7 0.7 fusion
  (3 shorter events, 0.1 us)
Async XLA Ops:
  0.0 3.4 %copy-start = (bf16[4,128,8]{1,2,0:T(8,128)(2,1)S(1)}, bf16[4,128,8]{1,2,0:T(8,128)(2,1)}, u32[]{:S(2)}) copy-start(bf16[4,128,8]{1,2,0:T(8,128)(2,1)} %param.4) | copy-start | bytes 24580
  0.0 3.4 %collective-permute-start.1 = (bf16[4,8,128]{2,1,0:T(8,128)(2,1)}, bf16[4,8,128]{2,1,0:T(8,128)(2,1)S(1)}, u32[]{:S(2)}, u32[]{:S(2)}) collective-permute-start(bf16[4,8,128]{2,1,0:T(8,128)(2,1)} %bitcast.25), channel_id=1, source_target_pairs={{0,16},{16,0},{1,17},{17,1},{2,18},{18,2},{3,19},{19,3},{4,20},{20... | collective-permute-start | bytes 24584 | tf_op jit(solution)/shard_map/ppermute | solution.py:220
  4.2 28.7 %all-to-all-start = ((bf16[16,2,4,8,128]{4,3,2,1,0:T(8,128)(2,1)}), bf16[16,2,4,8,128]{4,3,2,1,0:T(8,128)(2,1)S(1)}, u32[]{:S(2)}, u32[]{:S(2)}) async-start(bf16[16,2,4,8,128]{4,3,2,1,0:T(8,128)(2,1)} %broadcast_in_dim.4), calls=%async_computation | async-start | bytes 524288 | tf_op jit(solution)/shard_map/all_to_all | solution.py:232
  33.7 7.6 %copy-start.1 = (bf16[256,256]{1,0:T(8,128)(2,1)S(1)}, bf16[256,256]{1,0:T(8,128)(2,1)}, u32[]{:S(2)}) copy-start(bf16[256,256]{1,0:T(8,128)(2,1)} %param.5) | copy-start | bytes 393220
  33.7 8.3 %copy-start.2 = (bf16[128,256]{1,0:T(8,128)(2,1)S(1)}, bf16[128,256]{1,0:T(8,128)(2,1)}, u32[]{:S(2)}) copy-start(bf16[128,256]{1,0:T(8,128)(2,1)} %param.3) | copy-start | bytes 196612
  33.7 19.7 %all-to-all-start.1 = ((bf16[16,112,128]{2,1,0:T(8,128)(2,1)}), bf16[16,112,128]{2,1,0:T(8,128)(2,1)S(1)}, u32[]{:S(2)}, u32[]{:S(2)}) async-start(bf16[16,112,128]{2,1,0:T(8,128)(2,1)} %windows.1), calls=%async_computation.1 | async-start | bytes 917504 | tf_op jit(solution)/shard_map/all_to_all | solution.py:239
  41.3 4.5 %collective-permute-start.2 = (bf16[256,256]{1,0:T(8,128)(2,1)S(1)}, bf16[256,256]{1,0:T(8,128)(2,1)S(1)}, u32[]{:S(2)}, u32[]{:S(2)}) collective-permute-start(bf16[256,256]{1,0:T(8,128)(2,1)S(1)} %copy-done.1), channel_id=1, source_target_pairs={{0,0},{1,1},{2,2},{3,3},{4,16},{5,17},{6,18},{7,19},{8,256},{9,257... | collective-permute-start | bytes 393224 | tf_op jit(solution)/shard_map/ppermute | solution.py:227
  42.0 11.4 %collective-permute-start = (bf16[128,256]{1,0:T(8,128)(2,1)S(1)}, bf16[128,256]{1,0:T(8,128)(2,1)S(1)}, u32[]{:S(2)}, u32[]{:S(2)}) collective-permute-start(bf16[128,256]{1,0:T(8,128)(2,1)S(1)} %copy-done.2), channel_id=1, source_target_pairs={{0,0},{1,64},{2,128},{3,192},{4,16},{5,80},{6,144},{7,208},{8,256}... | collective-permute-start | bytes 196616 | tf_op jit(solution)/shard_map/ppermute | solution.py:228
  45.9 26.2 %collective-permute-start.3 = (bf16[256,256]{1,0:T(8,128)(2,1)S(1)}, bf16[256,256]{1,0:T(8,128)(2,1)S(1)}, u32[]{:S(2)}, u32[]{:S(2)}) collective-permute-start(bf16[256,256]{1,0:T(8,128)(2,1)S(1)} %collective-permute-done.2), channel_id=1, source_target_pairs={{0,4},{4,0},{8,12},{12,8},{1,5},{5,1},{9,13},{13,9},{2,6},{6,2},{1... | collective-permute-start | bytes 393224 | tf_op jit(solution)/shard_map/ppermute | solution.py:220
  63.9 57.5 %all-to-all-start.2 = ((bf16[8,128,256]{2,1,0:T(8,128)(2,1)}), bf16[8,128,256]{2,1,0:T(8,128)(2,1)S(1)}, u32[]{:S(2)}, u32[]{:S(2)}) async-start(bf16[8,128,256]{2,1,0:T(8,128)(2,1)} %broadcast_in_dim.5), calls=%async_computation.2 | async-start | bytes 1048576 | tf_op jit(solution)/shard_map/all_to_all | solution.py:241
  72.1 16.7 %collective-permute-start.4 = (bf16[2,256,256]{2,1,0:T(8,128)(2,1)S(1)}, bf16[2,256,256]{2,1,0:T(8,128)(2,1)S(1)}, u32[]{:S(2)}, u32[]{:S(2)}) collective-permute-start(bf16[2,256,256]{2,1,0:T(8,128)(2,1)S(1)} %pad_maximum_fusion.1), channel_id=1, source_target_pairs={{0,8},{4,12},{8,0},{12,4},{1,9},{5,13},{9,1},{13,5},{2,10},{6,14},... | collective-permute-start | bytes 786440 | tf_op jit(solution)/shard_map/ppermute | solution.py:220
  88.9 16.7 %collective-permute-start.5 = (bf16[4,256,256]{2,1,0:T(8,128)(2,1)S(1)}, bf16[4,256,256]{2,1,0:T(8,128)(2,1)S(1)}, u32[]{:S(2)}, u32[]{:S(2)}) collective-permute-start(bf16[4,256,256]{2,1,0:T(8,128)(2,1)S(1)} %pad_maximum_fusion.w0_ref), channel_id=1, source_target_pairs={{0,1},{1,0},{2,3},{3,2},{4,5},{5,4},{6,7},{7,6},{8,9},{9,8},{10,11... | collective-permute-start | bytes 1572872 | tf_op jit(solution)/shard_map/ppermute | solution.py:220
  91.3 23.3 %collective-permute-start.6 = (bf16[4,256,256]{2,1,0:T(8,128)(2,1)S(1)}, bf16[4,256,256]{2,1,0:T(8,128)(2,1)S(1)}, u32[]{:S(2)}, u32[]{:S(2)}) collective-permute-start(bf16[4,256,256]{2,1,0:T(8,128)(2,1)S(1)} %pad_maximum_fusion.w0_ref), channel_id=1, source_target_pairs={{0,2},{1,3},{2,0},{3,1},{4,6},{5,7},{6,4},{7,5},{8,10},{9,11},{10,... | collective-permute-start | bytes 1572872 | tf_op jit(solution)/shard_map/ppermute | solution.py:220
  95.1 26.3 %collective-permute-start.7 = (bf16[4,256,256]{2,1,0:T(8,128)(2,1)S(1)}, bf16[4,256,256]{2,1,0:T(8,128)(2,1)S(1)}, u32[]{:S(2)}, u32[]{:S(2)}) collective-permute-start(bf16[4,256,256]{2,1,0:T(8,128)(2,1)S(1)} %pad_maximum_fusion.w0_ref), channel_id=1, source_target_pairs={{0,3},{1,2},{2,1},{3,0},{4,7},{5,6},{6,5},{7,4},{8,11},{9,10},{10,... | collective-permute-start | bytes 1572872 | tf_op jit(solution)/shard_map/ppermute | solution.py:220
  123.4 4.0 %collective-permute-start.8 = (f32[2,256,256]{2,1,0:T(8,128)}, f32[2,256,256]{2,1,0:T(8,128)S(1)}, u32[]{:S(2)}, u32[]{:S(2)}) collective-permute-start(f32[2,256,256]{2,1,0:T(8,128)} %get-tuple-element.8), channel_id=1, source_target_pairs={{0,16},{16,0},{1,17},{17,1},{2,18},{18,2},{3,19},{19,3},{4,20},{20... | collective-permute-start | bytes 1572872 | tf_op jit(solution)/shard_map/ppermute | solution.py:220
  127.5 18.2 %collective-permute-start.9 = (bf16[256,256]{1,0:T(8,128)(2,1)S(1)}, bf16[256,256]{1,0:T(8,128)(2,1)S(1)}, u32[]{:S(2)}, u32[]{:S(2)}) collective-permute-start(bf16[256,256]{1,0:T(8,128)(2,1)S(1)} %fusion.1), channel_id=1, source_target_pairs={{0,256},{256,0},{1,257},{257,1},{2,258},{258,2},{3,259},{259,3},{4... | collective-permute-start | bytes 393224 | tf_op jit(solution)/shard_map/ppermute | solution.py:220

commit v4 on v3

--- a/solution.py
+++ b/solution.py
@@ -132,7 +132,9 @@
         return carry
 
     lax.fori_loop(0, steps // 2, step, 0)
-    out_ref[...] = acc_ref[...].astype(BF16)
+    done = acc_ref[...].astype(BF16)
+    for receiver in range(8):
+        out_ref[receiver] = done
 
 
 def window_kernel(parity_ref, all_ref, out_ref):
@@ -164,7 +166,7 @@
 def attend(block, queries, window):
     return pl.pallas_call(
         attend_kernel,
-        out_shape=jax.ShapeDtypeStruct((BLOCK, 2 * HD), BF16),
+        out_shape=jax.ShapeDtypeStruct((8, BLOCK, 2 * HD), BF16),
         in_specs=[
             pl.BlockSpec(memory_space=pltpu.SMEM),
             pl.BlockSpec(memory_space=pltpu.VMEM),
@@ -230,15 +232,17 @@
     other = across(raw, "core", 1)
     pair = jnp.where(core == 0, jnp.stack([raw, other]), jnp.stack([other, raw]))
     everything = lax.all_to_all(jnp.broadcast_to(pair[None], (16,) + pair.shape), ("yh", "z"), 0, 0)
-    columns = jnp.stack([moved, across(moved, "yl", 1)])
-    columns = jnp.concatenate([columns, across(columns, "yl", 2)])
+    columns = [moved]
+    for away in (1, 2, 3):
+        columns.append(across(moved, "yl", away))
+    columns = jnp.stack(columns)
     weights = [columns]
     for away in (1, 2, 3):
         weights.append(across(columns, "x", away))
     window = windows_of(parity.reshape(1), everything.reshape(32, 4, 8, 128))
     window = lax.all_to_all(window, HEAD, 0, 0)
     attention = attend(block.reshape(1), queries, window)
-    attention = lax.all_to_all(jnp.broadcast_to(attention[None], (8,) + attention.shape), "z", 0, 0)
+    attention = lax.all_to_all(attention, "z", 0, 0)
     keep, send = project(jnp.stack([core, yl, x]), attention.reshape(4, 256, 256), weights)
     got = across(send, "core", 1)
     summed = keep + got

time: 147 us -> 156 us (1.061)
  the two profiles are of different devices: /device:TPU:6 before, /device:TPU:15 now
where the time goes in v4:
time: 156 us
  waiting for transfers between devices  73.4 us (47%)
  starting transfers between devices  67 us (43%)
  Pallas kernels  13.3 us (9%)
    ppermute x9, waiting for transfers between devices, across(): return lax.ppermute(x, axis, [(i, i ^ away) for i in range(count)])  45.6 us
    ppermute x9, starting transfers between devices, across(): return lax.ppermute(x, axis, [(i, i ^ away) for i in range(count)])  39.3 us
    all_to_all x1, waiting for transfers between devices, layer(): lax.all_to_all(jnp.broadcast_to(pair[None], (16,) + pair.shape), ('yh', '...  15 us
    all_to_all x1, starting transfers between devices, layer(): lax.all_to_all(jnp.broadcast_to(pair[None], (16,) + pair.shape), ('yh', '...  14.5 us
    ppermute x1, waiting for transfers between devices, layer(): queries = lax.ppermute(queries, ALL, attention_pairs())  12.8 us
    pallas_call x1, Pallas kernels, attend(): pl.pallas_call(attend_kernel, out_shape=jax.ShapeDtypeStruct((8, BLOCK, 2...  10.4 us
    all_to_all x1, starting transfers between devices, layer(): window = lax.all_to_all(window, HEAD, 0, 0)  5.26 us
    ppermute x1, starting transfers between devices, layer(): queries = lax.ppermute(queries, ALL, attention_pairs())  3.65 us
  transfers between devices with their start and end apart: 14, of which 10 were waited for; matrix products, arithmetic and copies ran while one was open for 0% of the time, Pallas kernels for 0%

profile of v4, /device:TPU:15, one launch (start us, length us, event | category | flops | bytes accessed | tf_op | source)
XLA Modules:
  0.0 155.7 jit_solution(13838118777906336199)
XLA Ops:
  0.0 0.0 copy-start
  0.0 2.7 %collective-permute-start.1 = (bf16[4,8,128]{2,1,0:T(8,128)(2,1)}, bf16[4,8,128]{2,1,0:T(8,128)(2,1)S(1)}, u32[]{:S(2)}, u32[]{:S(2)}) collective-permute-start(bf16[4,8,128]{2,1,0:T(8,128)(2,1)} %bitcast.27), channel_id=1, source_target_pairs={{0,16},{16,0},{1,17},{17,1},{2,18},{18,2},{3,19},{19,3},{4,20},{20... | collective-permute-start | bytes 24584 | tf_op jit(solution)/shard_map/ppermute | solution.py:222
  2.7 1.0 collective-permute-done.1
  3.7 0.0 copy-done
  3.7 0.8 broadcast_in_dim.2
  4.5 14.5 %all-to-all-start = ((bf16[16,2,4,8,128]{4,3,2,1,0:T(8,128)(2,1)}), bf16[16,2,4,8,128]{4,3,2,1,0:T(8,128)(2,1)S(1)}, u32[]{:S(2)}, u32[]{:S(2)}) async-start(bf16[16,2,4,8,128]{4,3,2,1,0:T(8,128)(2,1)} %broadcast_in_dim.2), calls=%async_computation | async-start | bytes 524288 | tf_op jit(solution)/shard_map/all_to_all | solution.py:234
  19.0 15.0 %all-to-all-done = bf16[16,2,4,8,128]{4,3,2,1,0:T(8,128)(2,1)S(1)} async-done(((bf16[16,2,4,8,128]{4,3,2,1,0:T(8,128)(2,1)}), bf16[16,2,4,8,128]{4,3,2,1,0:T(8,128)(2,1)S(1)}, u32[]{:S(2)}, u32[]{:S(2)}) %all-to-all-start) | async-done | bytes 262176 | tf_op jit(solution)/shard_map/all_to_all | solution.py:234
  34.0 0.8 windows.1
  34.9 0.0 copy-start.2
  34.9 5.3 %all-to-all-start.1 = ((bf16[16,112,128]{2,1,0:T(8,128)(2,1)}), bf16[16,112,128]{2,1,0:T(8,128)(2,1)S(1)}, u32[]{:S(2)}, u32[]{:S(2)}) async-start(bf16[16,112,128]{2,1,0:T(8,128)(2,1)} %windows.1), calls=%async_computation.1 | async-start | bytes 917504 | tf_op jit(solution)/shard_map/all_to_all | solution.py:243
  40.1 0.0 copy-done.2
  40.1 3.6 %collective-permute-start = (bf16[128,256]{1,0:T(8,128)(2,1)S(1)}, bf16[128,256]{1,0:T(8,128)(2,1)S(1)}, u32[]{:S(2)}, u32[]{:S(2)}) collective-permute-start(bf16[128,256]{1,0:T(8,128)(2,1)S(1)} %copy-done.2), channel_id=1, source_target_pairs={{0,0},{1,64},{2,128},{3,192},{4,16},{5,80},{6,144},{7,208},{8,256}... | collective-permute-start | bytes 196616 | tf_op jit(solution)/shard_map/ppermute | solution.py:230
  43.8 12.8 %collective-permute-done.q_ref = bf16[128,256]{1,0:T(8,128)(2,1)S(1)} collective-permute-done((bf16[128,256]{1,0:T(8,128)(2,1)S(1)}, bf16[128,256]{1,0:T(8,128)(2,1)S(1)}, u32[]{:S(2)}, u32[]{:S(2)}) %collective-permute-start) | collective-permute-done | bytes 65568 | tf_op jit(solution)/shard_map/ppermute | solution.py:230
  56.6 0.0 all-to-all-done.1.kv_ref
  56.7 10.4 %attend.1 = bf16[8,128,256]{2,1,0:T(8,128)(2,1)} custom-call(s32[1]{0:T(128)} %bitcast.3.where_ref, bf16[128,256]{1,0:T(8,128)(2,1)S(1)} %collective-permute-done.q_ref, bf16[16,112,128]{2,1,0:T(8,128)(2,1)S(1)} %all-to-all-done.1.kv_ref), custom_call_target="tpu_custom_call" | custom-call | flops 6000000000 | bytes 1000000 | tf_op jit(solution)/shard_map/attend/pallas_call | solution.py:167
  67.1 0.0 copy-start.1
  67.1 3.6 %all-to-all-start.2 = ((bf16[8,128,256]{2,1,0:T(8,128)(2,1)}), bf16[8,128,256]{2,1,0:T(8,128)(2,1)S(1)}, u32[]{:S(2)}, u32[]{:S(2)}) async-start(bf16[8,128,256]{2,1,0:T(8,128)(2,1)} %attend.1), calls=%async_computation.2 | async-start | bytes 1048576 | tf_op jit(solution)/shard_map/all_to_all | solution.py:245
  70.7 0.0 copy-done.1
  70.7 0.7 collective-permute-start.2
  71.4 0.0 collective-permute-done.2
  71.4 5.6 %collective-permute-start.3 = (bf16[256,256]{1,0:T(8,128)(2,1)S(1)}, bf16[256,256]{1,0:T(8,128)(2,1)S(1)}, u32[]{:S(2)}, u32[]{:S(2)}) collective-permute-start(bf16[256,256]{1,0:T(8,128)(2,1)S(1)} %collective-permute-done.2), channel_id=1, source_target_pairs={{0,4},{4,0},{8,12},{12,8},{1,5},{5,1},{9,13},{13,9},{2,6},{6,2},{1... | collective-permute-start | bytes 393224 | tf_op jit(solution)/shard_map/ppermute | solution.py:222
  77.0 10.5 %collective-permute-start.4 = (bf16[256,256]{1,0:T(8,128)(2,1)S(1)}, bf16[256,256]{1,0:T(8,128)(2,1)S(1)}, u32[]{:S(2)}, u32[]{:S(2)}) collective-permute-start(bf16[256,256]{1,0:T(8,128)(2,1)S(1)} %collective-permute-done.2), channel_id=1, source_target_pairs={{0,8},{4,12},{8,0},{12,4},{1,9},{5,13},{9,1},{13,5},{2,10},{6,14},... | collective-permute-start | bytes 393224 | tf_op jit(solution)/shard_map/ppermute | solution.py:222
  87.5 1.9 %collective-permute-start.5 = (bf16[256,256]{1,0:T(8,128)(2,1)S(1)}, bf16[256,256]{1,0:T(8,128)(2,1)S(1)}, u32[]{:S(2)}, u32[]{:S(2)}) collective-permute-start(bf16[256,256]{1,0:T(8,128)(2,1)S(1)} %collective-permute-done.2), channel_id=1, source_target_pairs={{0,12},{4,8},{8,4},{12,0},{1,13},{5,9},{9,5},{13,1},{2,14},{6,10},... | collective-permute-start | bytes 393224 | tf_op jit(solution)/shard_map/ppermute | solution.py:222
  89.5 0.0 collective-permute-done.3
  89.5 1.1 collective-permute-done.4
  90.6 8.6 %collective-permute-done.5 = bf16[256,256]{1,0:T(8,128)(2,1)S(1)} collective-permute-done((bf16[256,256]{1,0:T(8,128)(2,1)S(1)}, bf16[256,256]{1,0:T(8,128)(2,1)S(1)}, u32[]{:S(2)}, u32[]{:S(2)}) %collective-permute-start.5) | collective-permute-done | bytes 131104 | tf_op jit(solution)/shard_map/ppermute | solution.py:222
  99.1 0.1 pad_maximum_fusion.w0_ref
  99.2 3.3 %collective-permute-start.6 = (bf16[4,256,256]{2,1,0:T(8,128)(2,1)S(1)}, bf16[4,256,256]{2,1,0:T(8,128)(2,1)S(1)}, u32[]{:S(2)}, u32[]{:S(2)}) collective-permute-start(bf16[4,256,256]{2,1,0:T(8,128)(2,1)S(1)} %pad_maximum_fusion.w0_ref), channel_id=1, source_target_pairs={{0,1},{1,0},{2,3},{3,2},{4,5},{5,4},{6,7},{7,6},{8,9},{9,8},{10,11... | collective-permute-start | bytes 1572872 | tf_op jit(solution)/shard_map/ppermute | solution.py:222
  102.5 4.5 %collective-permute-start.7 = (bf16[4,256,256]{2,1,0:T(8,128)(2,1)S(1)}, bf16[4,256,256]{2,1,0:T(8,128)(2,1)S(1)}, u32[]{:S(2)}, u32[]{:S(2)}) collective-permute-start(bf16[4,256,256]{2,1,0:T(8,128)(2,1)S(1)} %pad_maximum_fusion.w0_ref), channel_id=1, source_target_pairs={{0,2},{1,3},{2,0},{3,1},{4,6},{5,7},{6,4},{7,5},{8,10},{9,11},{10,... | collective-permute-start | bytes 1572872 | tf_op jit(solution)/shard_map/ppermute | solution.py:222
  107.0 1.9 %collective-permute-start.8 = (bf16[4,256,256]{2,1,0:T(8,128)(2,1)S(1)}, bf16[4,256,256]{2,1,0:T(8,128)(2,1)S(1)}, u32[]{:S(2)}, u32[]{:S(2)}) collective-permute-start(bf16[4,256,256]{2,1,0:T(8,128)(2,1)S(1)} %pad_maximum_fusion.w0_ref), channel_id=1, source_target_pairs={{0,3},{1,2},{2,1},{3,0},{4,7},{5,6},{6,5},{7,4},{8,11},{9,10},{10,... | collective-permute-start | bytes 1572872 | tf_op jit(solution)/shard_map/ppermute | solution.py:222
  108.9 0.1 pad_add_fusion.place_ref
  109.0 4.5 %collective-permute-done.6.w1_ref = bf16[4,256,256]{2,1,0:T(8,128)(2,1)S(1)} collective-permute-done((bf16[4,256,256]{2,1,0:T(8,128)(2,1)S(1)}, bf16[4,256,256]{2,1,0:T(8,128)(2,1)S(1)}, u32[]{:S(2)}, u32[]{:S(2)}) %collective-permute-start.6) | collective-permute-done | bytes 524320 | tf_op jit(solution)/shard_map/ppermute | solution.py:222
  113.5 14.0 %collective-permute-done.7.w2_ref = bf16[4,256,256]{2,1,0:T(8,128)(2,1)S(1)} collective-permute-done((bf16[4,256,256]{2,1,0:T(8,128)(2,1)S(1)}, bf16[4,256,256]{2,1,0:T(8,128)(2,1)S(1)}, u32[]{:S(2)}, u32[]{:S(2)}) %collective-permute-start.7) | collective-permute-done | bytes 524320 | tf_op jit(solution)/shard_map/ppermute | solution.py:222
  127.5 5.9 %collective-permute-done.8.w3_ref = bf16[4,256,256]{2,1,0:T(8,128)(2,1)S(1)} collective-permute-done((bf16[4,256,256]{2,1,0:T(8,128)(2,1)S(1)}, bf16[4,256,256]{2,1,0:T(8,128)(2,1)S(1)}, u32[]{:S(2)}, u32[]{:S(2)}) %collective-permute-start.8) | collective-permute-done | bytes 524320 | tf_op jit(solution)/shard_map/ppermute | solution.py:222
  133.4 0.0 all-to-all-done.2
  133.4 2.1 %project.1 = (f32[2,256,256]{2,1,0:T(8,128)S(1)}, f32[2,256,256]{2,1,0:T(8,128)}) custom-call(s32[3]{0:T(128)S(1)} %pad_add_fusion.place_ref, bf16[4,256,256]{2,1,0:T(8,128)(2,1)S(1)} %bitcast.21, bf16[4,256,256]{2,1,0:T(8,128)(2,1)S(1)} %pad_maximum_fusion.w0_ref, bf16[4,256,256]{2,1,0:T(8,128)(2,1)S(1)} %collective-permute-done.6.w1_ref, ...), custom_call_target="tpu_custom_call" | custom-call | flops 540000000 | bytes 4000000 | tf_op jit(solution)/shard_map/project/pallas_call | solution.py:209
  135.4 4.2 %collective-permute-start.9 = (f32[2,256,256]{2,1,0:T(8,128)}, f32[2,256,256]{2,1,0:T(8,128)S(1)}, u32[]{:S(2)}, u32[]{:S(2)}) collective-permute-start(f32[2,256,256]{2,1,0:T(8,128)} %get-tuple-element.8), channel_id=1, source_target_pairs={{0,16},{16,0},{1,17},{17,1},{2,18},{18,2},{3,19},{19,3},{4,20},{20... | collective-permute-start | bytes 1572872 | tf_op jit(solution)/shard_map/ppermute | solution.py:222
  139.6 1.7 %collective-permute-done.9 = f32[2,256,256]{2,1,0:T(8,128)S(1)} collective-permute-done((f32[2,256,256]{2,1,0:T(8,128)}, f32[2,256,256]{2,1,0:T(8,128)S(1)}, u32[]{:S(2)}, u32[]{:S(2)}) %collective-permute-start.9) | collective-permute-done | bytes 524320 | tf_op jit(solution)/shard_map/ppermute | solution.py:222
  141.3 0.1 add.27
  141.4 4.8 %collective-permute-start.10 = (bf16[256,256]{1,0:T(8,128)(2,1)S(1)}, bf16[256,256]{1,0:T(8,128)(2,1)S(1)}, u32[]{:S(2)}, u32[]{:S(2)}) collective-permute-start(bf16[256,256]{1,0:T(8,128)(2,1)S(1)} %fusion.1), channel_id=1, source_target_pairs={{0,256},{256,0},{1,257},{257,1},{2,258},{258,2},{3,259},{259,3},{4... | collective-permute-start | bytes 393224 | tf_op jit(solution)/shard_map/ppermute | solution.py:222
  146.2 8.8 %collective-permute-done.10 = bf16[256,256]{1,0:T(8,128)(2,1)S(1)} collective-permute-done((bf16[256,256]{1,0:T(8,128)(2,1)S(1)}, bf16[256,256]{1,0:T(8,128)(2,1)S(1)}, u32[]{:S(2)}, u32[]{:S(2)}) %collective-permute-start.10) | collective-permute-done | bytes 131104 | tf_op jit(solution)/shard_map/ppermute | solution.py:222
  155.0 0.7 fusion
  (2 shorter events, 0.0 us)
Async XLA Ops:
  0.0 3.7 %copy-start = (bf16[4,128,8]{1,2,0:T(8,128)(2,1)S(1)}, bf16[4,128,8]{1,2,0:T(8,128)(2,1)}, u32[]{:S(2)}) copy-start(bf16[4,128,8]{1,2,0:T(8,128)(2,1)} %param.4) | copy-start | bytes 24580
  0.0 3.7 %collective-permute-start.1 = (bf16[4,8,128]{2,1,0:T(8,128)(2,1)}, bf16[4,8,128]{2,1,0:T(8,128)(2,1)S(1)}, u32[]{:S(2)}, u32[]{:S(2)}) collective-permute-start(bf16[4,8,128]{2,1,0:T(8,128)(2,1)} %bitcast.27), channel_id=1, source_target_pairs={{0,16},{16,0},{1,17},{17,1},{2,18},{18,2},{3,19},{19,3},{4,20},{20... | collective-permute-start | bytes 24584 | tf_op jit(solution)/shard_map/ppermute | solution.py:222
  4.5 29.5 %all-to-all-start = ((bf16[16,2,4,8,128]{4,3,2,1,0:T(8,128)(2,1)}), bf16[16,2,4,8,128]{4,3,2,1,0:T(8,128)(2,1)S(1)}, u32[]{:S(2)}, u32[]{:S(2)}) async-start(bf16[16,2,4,8,128]{4,3,2,1,0:T(8,128)(2,1)} %broadcast_in_dim.2), calls=%async_computation | async-start | bytes 524288 | tf_op jit(solution)/shard_map/all_to_all | solution.py:234
  34.9 5.3 %copy-start.2 = (bf16[128,256]{1,0:T(8,128)(2,1)S(1)}, bf16[128,256]{1,0:T(8,128)(2,1)}, u32[]{:S(2)}) copy-start(bf16[128,256]{1,0:T(8,128)(2,1)} %param.3) | copy-start | bytes 196612
  34.9 21.8 %all-to-all-start.1 = ((bf16[16,112,128]{2,1,0:T(8,128)(2,1)}), bf16[16,112,128]{2,1,0:T(8,128)(2,1)S(1)}, u32[]{:S(2)}, u32[]{:S(2)}) async-start(bf16[16,112,128]{2,1,0:T(8,128)(2,1)} %windows.1), calls=%async_computation.1 | async-start | bytes 917504 | tf_op jit(solution)/shard_map/all_to_all | solution.py:243
  40.1 16.5 %collective-permute-start = (bf16[128,256]{1,0:T(8,128)(2,1)S(1)}, bf16[128,256]{1,0:T(8,128)(2,1)S(1)}, u32[]{:S(2)}, u32[]{:S(2)}) collective-permute-start(bf16[128,256]{1,0:T(8,128)(2,1)S(1)} %copy-done.2), channel_id=1, source_target_pairs={{0,0},{1,64},{2,128},{3,192},{4,16},{5,80},{6,144},{7,208},{8,256}... | collective-permute-start | bytes 196616 | tf_op jit(solution)/shard_map/ppermute | solution.py:230
  67.1 3.6 %copy-start.1 = (bf16[256,256]{1,0:T(8,128)(2,1)S(1)}, bf16[256,256]{1,0:T(8,128)(2,1)}, u32[]{:S(2)}) copy-start(bf16[256,256]{1,0:T(8,128)(2,1)} %param.5) | copy-start | bytes 393220
  67.1 66.3 %all-to-all-start.2 = ((bf16[8,128,256]{2,1,0:T(8,128)(2,1)}), bf16[8,128,256]{2,1,0:T(8,128)(2,1)S(1)}, u32[]{:S(2)}, u32[]{:S(2)}) async-start(bf16[8,128,256]{2,1,0:T(8,128)(2,1)} %attend.1), calls=%async_computation.2 | async-start | bytes 1048576 | tf_op jit(solution)/shard_map/all_to_all | solution.py:245
  70.7 0.7 collective-permute-start.2
  71.4 18.0 %collective-permute-start.3 = (bf16[256,256]{1,0:T(8,128)(2,1)S(1)}, bf16[256,256]{1,0:T(8,128)(2,1)S(1)}, u32[]{:S(2)}, u32[]{:S(2)}) collective-permute-start(bf16[256,256]{1,0:T(8,128)(2,1)S(1)} %collective-permute-done.2), channel_id=1, source_target_pairs={{0,4},{4,0},{8,12},{12,8},{1,5},{5,1},{9,13},{13,9},{2,6},{6,2},{1... | collective-permute-start | bytes 393224 | tf_op jit(solution)/shard_map/ppermute | solution.py:222
  77.0 13.6 %collective-permute-start.4 = (bf16[256,256]{1,0:T(8,128)(2,1)S(1)}, bf16[256,256]{1,0:T(8,128)(2,1)S(1)}, u32[]{:S(2)}, u32[]{:S(2)}) collective-permute-start(bf16[256,256]{1,0:T(8,128)(2,1)S(1)} %collective-permute-done.2), channel_id=1, source_target_pairs={{0,8},{4,12},{8,0},{12,4},{1,9},{5,13},{9,1},{13,5},{2,10},{6,14},... | collective-permute-start | bytes 393224 | tf_op jit(solution)/shard_map/ppermute | solution.py:222
  87.5 11.6 %collective-permute-start.5 = (bf16[256,256]{1,0:T(8,128)(2,1)S(1)}, bf16[256,256]{1,0:T(8,128)(2,1)S(1)}, u32[]{:S(2)}, u32[]{:S(2)}) collective-permute-start(bf16[256,256]{1,0:T(8,128)(2,1)S(1)} %collective-permute-done.2), channel_id=1, source_target_pairs={{0,12},{4,8},{8,4},{12,0},{1,13},{5,9},{9,5},{13,1},{2,14},{6,10},... | collective-permute-start | bytes 393224 | tf_op jit(solution)/shard_map/ppermute | solution.py:222
  99.2 14.3 %collective-permute-start.6 = (bf16[4,256,256]{2,1,0:T(8,128)(2,1)S(1)}, bf16[4,256,256]{2,1,0:T(8,128)(2,1)S(1)}, u32[]{:S(2)}, u32[]{:S(2)}) collective-permute-start(bf16[4,256,256]{2,1,0:T(8,128)(2,1)S(1)} %pad_maximum_fusion.w0_ref), channel_id=1, source_target_pairs={{0,1},{1,0},{2,3},{3,2},{4,5},{5,4},{6,7},{7,6},{8,9},{9,8},{10,11... | collective-permute-start | bytes 1572872 | tf_op jit(solution)/shard_map/ppermute | solution.py:222
  102.5 25.0 %collective-permute-start.7 = (bf16[4,256,256]{2,1,0:T(8,128)(2,1)S(1)}, bf16[4,256,256]{2,1,0:T(8,128)(2,1)S(1)}, u32[]{:S(2)}, u32[]{:S(2)}) collective-permute-start(bf16[4,256,256]{2,1,0:T(8,128)(2,1)S(1)} %pad_maximum_fusion.w0_ref), channel_id=1, source_target_pairs={{0,2},{1,3},{2,0},{3,1},{4,6},{5,7},{6,4},{7,5},{8,10},{9,11},{10,... | collective-permute-start | bytes 1572872 | tf_op jit(solution)/shard_map/ppermute | solution.py:222
  107.0 26.4 %collective-permute-start.8 = (bf16[4,256,256]{2,1,0:T(8,128)(2,1)S(1)}, bf16[4,256,256]{2,1,0:T(8,128)(2,1)S(1)}, u32[]{:S(2)}, u32[]{:S(2)}) collective-permute-start(bf16[4,256,256]{2,1,0:T(8,128)(2,1)S(1)} %pad_maximum_fusion.w0_ref), channel_id=1, source_target_pairs={{0,3},{1,2},{2,1},{3,0},{4,7},{5,6},{6,5},{7,4},{8,11},{9,10},{10,... | collective-permute-start | bytes 1572872 | tf_op jit(solution)/shard_map/ppermute | solution.py:222
  135.4 5.9 %collective-permute-start.9 = (f32[2,256,256]{2,1,0:T(8,128)}, f32[2,256,256]{2,1,0:T(8,128)S(1)}, u32[]{:S(2)}, u32[]{:S(2)}) collective-permute-start(f32[2,256,256]{2,1,0:T(8,128)} %get-tuple-element.8), channel_id=1, source_target_pairs={{0,16},{16,0},{1,17},{17,1},{2,18},{18,2},{3,19},{19,3},{4,20},{20... | collective-permute-start | bytes 1572872 | tf_op jit(solution)/shard_map/ppermute | solution.py:222
  141.4 13.6 %collective-permute-start.10 = (bf16[256,256]{1,0:T(8,128)(2,1)S(1)}, bf16[256,256]{1,0:T(8,128)(2,1)S(1)}, u32[]{:S(2)}, u32[]{:S(2)}) collective-permute-start(bf16[256,256]{1,0:T(8,128)(2,1)S(1)} %fusion.1), channel_id=1, source_target_pairs={{0,256},{256,0},{1,257},{257,1},{2,258},{258,2},{3,259},{259,3},{4... | collective-permute-start | bytes 393224 | tf_op jit(solution)/shard_map/ppermute | solution.py:222

commit v5 on v4

--- a/solution.py
+++ b/solution.py
@@ -41,9 +41,9 @@
     ]
 
 
-def weight_pairs():
+def weight_pairs(away):
     return [
-        (flat(yh, z, core, yl, x), flat(yl // 2, z, yl % 2, 2 * yh + core, x))
+        (flat(yh, z, core, yl, x), flat(yl // 2, z, yl % 2, (2 * yh + core) ^ away, x))
         for yh, z, core, yl, x in places()
     ]
 
@@ -226,16 +226,15 @@
     yh, z, core, yl, x = (lax.axis_index(name).astype(jnp.int32) for name in ALL)
     parity = z % 2
     block = 2 * (4 * yl + x) + parity
-    moved = lax.ppermute(w_out, ALL, weight_pairs())
+    moved = lax.ppermute(w_out, ALL, weight_pairs(0))
     queries = lax.ppermute(queries, ALL, attention_pairs())
     raw = jnp.transpose(kv, (0, 2, 1))
     other = across(raw, "core", 1)
     pair = jnp.where(core == 0, jnp.stack([raw, other]), jnp.stack([other, raw]))
     everything = lax.all_to_all(jnp.broadcast_to(pair[None], (16,) + pair.shape), ("yh", "z"), 0, 0)
-    columns = [moved]
-    for away in (1, 2, 3):
-        columns.append(across(moved, "yl", away))
-    columns = jnp.stack(columns)
+    columns = jnp.stack([moved, lax.ppermute(w_out, ALL, weight_pairs(2))])
+    across_row = across(columns, "yl", 1)
+    columns = jnp.stack([columns[0], across_row[0], columns[1], across_row[1]])
     weights = [columns]
     for away in (1, 2, 3):
         weights.append(across(columns, "x", away))

time: 156 us -> 134 us (0.86)
  the two profiles are of different devices: /device:TPU:15 before, /device:TPU:48 now
where the time goes in v5:
time: 134 us; the launch traced here: 133 us
  starting transfers between devices  62.9 us (47%)
  waiting for transfers between devices  55.2 us (41%)
  Pallas kernels  13.3 us (10%)
    ppermute x7, waiting for transfers between devices, across(): return lax.ppermute(x, axis, [(i, i ^ away) for i in range(count)])  35.3 us
    ppermute x7, starting transfers between devices, across(): return lax.ppermute(x, axis, [(i, i ^ away) for i in range(count)])  22.7 us
    all_to_all x1, starting transfers between devices, layer(): lax.all_to_all(jnp.broadcast_to(pair[None], (16,) + pair.shape), ('yh', '...  15.7 us
    pallas_call x1, Pallas kernels, attend(): pl.pallas_call(attend_kernel, out_shape=jax.ShapeDtypeStruct((8, BLOCK, 2...  10.5 us
    all_to_all x1, waiting for transfers between devices, layer(): lax.all_to_all(jnp.broadcast_to(pair[None], (16,) + pair.shape), ('yh', '...  10.5 us
    ppermute x1, waiting for transfers between devices, layer(): columns = jnp.stack([moved, lax.ppermute(w_out, ALL, weight_pairs(2))])  9.42 us
    ppermute x1, starting transfers between devices, layer(): columns = jnp.stack([moved, lax.ppermute(w_out, ALL, weight_pairs(2))])  8.85 us
    all_to_all x1, starting transfers between devices, layer(): attention = lax.all_to_all(attention, 'z', 0, 0)  7.43 us
  transfers between devices with their start and end apart: 13, of which 8 were waited for; matrix products, arithmetic and copies ran while one was open for 0% of the time, Pallas kernels for 8%

profile of v5, /device:TPU:48, one launch (start us, length us, event | category | flops | bytes accessed | tf_op | source)
XLA Modules:
  0.0 133.3 jit_solution(3695578576998761408)
XLA Ops:
  0.0 0.0 copy-start
  0.0 2.0 %collective-permute-start.1 = (bf16[4,8,128]{2,1,0:T(8,128)(2,1)}, bf16[4,8,128]{2,1,0:T(8,128)(2,1)S(1)}, u32[]{:S(2)}, u32[]{:S(2)}) collective-permute-start(bf16[4,8,128]{2,1,0:T(8,128)(2,1)} %bitcast.25), channel_id=1, source_target_pairs={{0,16},{16,0},{1,17},{17,1},{2,18},{18,2},{3,19},{19,3},{4,20},{20... | collective-permute-start | bytes 24584 | tf_op jit(solution)/shard_map/ppermute | solution.py:222
  2.1 1.3 %collective-permute-done.1 = bf16[4,8,128]{2,1,0:T(8,128)(2,1)S(1)} collective-permute-done((bf16[4,8,128]{2,1,0:T(8,128)(2,1)}, bf16[4,8,128]{2,1,0:T(8,128)(2,1)S(1)}, u32[]{:S(2)}, u32[]{:S(2)}) %collective-permute-start.1) | collective-permute-done | bytes 8224 | tf_op jit(solution)/shard_map/ppermute | solution.py:222
  3.4 0.0 copy-done
  3.4 0.8 broadcast_in_dim.2
  4.2 15.7 %all-to-all-start = ((bf16[16,2,4,8,128]{4,3,2,1,0:T(8,128)(2,1)}), bf16[16,2,4,8,128]{4,3,2,1,0:T(8,128)(2,1)S(1)}, u32[]{:S(2)}, u32[]{:S(2)}) async-start(bf16[16,2,4,8,128]{4,3,2,1,0:T(8,128)(2,1)} %broadcast_in_dim.2), calls=%async_computation | async-start | bytes 524288 | tf_op jit(solution)/shard_map/all_to_all | solution.py:234
  19.9 10.5 %all-to-all-done = bf16[16,2,4,8,128]{4,3,2,1,0:T(8,128)(2,1)S(1)} async-done(((bf16[16,2,4,8,128]{4,3,2,1,0:T(8,128)(2,1)}), bf16[16,2,4,8,128]{4,3,2,1,0:T(8,128)(2,1)S(1)}, u32[]{:S(2)}, u32[]{:S(2)}) %all-to-all-start) | async-done | bytes 262176 | tf_op jit(solution)/shard_map/all_to_all | solution.py:234
  30.3 0.8 windows.1
  31.2 0.0 copy-start.1
  31.2 0.0 copy-start.2
  31.2 6.8 %all-to-all-start.1 = ((bf16[16,112,128]{2,1,0:T(8,128)(2,1)}), bf16[16,112,128]{2,1,0:T(8,128)(2,1)S(1)}, u32[]{:S(2)}, u32[]{:S(2)}) async-start(bf16[16,112,128]{2,1,0:T(8,128)(2,1)} %windows.1), calls=%async_computation.1 | async-start | bytes 917504 | tf_op jit(solution)/shard_map/all_to_all | solution.py:242
  38.0 0.0 copy-done.1
  38.0 0.7 collective-permute-start.2
  38.7 8.8 %collective-permute-start.3 = (bf16[256,256]{1,0:T(8,128)(2,1)S(1)}, bf16[256,256]{1,0:T(8,128)(2,1)S(1)}, u32[]{:S(2)}, u32[]{:S(2)}) collective-permute-start(bf16[256,256]{1,0:T(8,128)(2,1)S(1)} %copy-done.1), channel_id=1, source_target_pairs={{0,8},{1,9},{2,10},{3,11},{4,24},{5,25},{6,26},{7,27},{8,264},{9,2... | collective-permute-start | bytes 393224 | tf_op jit(solution)/shard_map/ppermute | solution.py:235
  47.5 0.0 copy-done.2
  47.5 0.7 collective-permute-start
  48.2 0.0 collective-permute-done.2
  48.2 9.4 %collective-permute-done.3 = bf16[256,256]{1,0:T(8,128)(2,1)S(1)} collective-permute-done((bf16[256,256]{1,0:T(8,128)(2,1)S(1)}, bf16[256,256]{1,0:T(8,128)(2,1)S(1)}, u32[]{:S(2)}, u32[]{:S(2)}) %collective-permute-start.3) | collective-permute-done | bytes 131104 | tf_op jit(solution)/shard_map/ppermute | solution.py:235
  57.7 2.4 %collective-permute-start.4 = (bf16[2,256,256]{2,1,0:T(8,128)(2,1)S(1)}, bf16[2,256,256]{2,1,0:T(8,128)(2,1)S(1)}, u32[]{:S(2)}, u32[]{:S(2)}) collective-permute-start(bf16[2,256,256]{2,1,0:T(8,128)(2,1)S(1)} %pad_maximum_fusion.1), channel_id=1, source_target_pairs={{0,4},{4,0},{8,12},{12,8},{1,5},{5,1},{9,13},{13,9},{2,6},{6,2},{1... | collective-permute-start | bytes 786440 | tf_op jit(solution)/shard_map/ppermute | solution.py:222
  60.0 0.0 collective-permute-done.q_ref
  60.0 0.0 all-to-all-done.1.kv_ref
  60.1 10.5 %attend.1 = bf16[8,128,256]{2,1,0:T(8,128)(2,1)} custom-call(s32[1]{0:T(128)} %bitcast.3.where_ref, bf16[128,256]{1,0:T(8,128)(2,1)S(1)} %collective-permute-done.q_ref, bf16[16,112,128]{2,1,0:T(8,128)(2,1)S(1)} %all-to-all-done.1.kv_ref), custom_call_target="tpu_custom_call" | custom-call | flops 6000000000 | bytes 1000000 | tf_op jit(solution)/shard_map/attend/pallas_call | solution.py:167
  70.5 7.4 %all-to-all-start.2 = ((bf16[8,128,256]{2,1,0:T(8,128)(2,1)}), bf16[8,128,256]{2,1,0:T(8,128)(2,1)S(1)}, u32[]{:S(2)}, u32[]{:S(2)}) async-start(bf16[8,128,256]{2,1,0:T(8,128)(2,1)} %attend.1), calls=%async_computation.2 | async-start | bytes 1048576 | tf_op jit(solution)/shard_map/all_to_all | solution.py:244
  77.9 0.0 collective-permute-done.4
  78.0 0.1 pad_maximum_fusion.w0_ref
  78.0 1.9 %collective-permute-start.5 = (bf16[4,256,256]{2,1,0:T(8,128)(2,1)S(1)}, bf16[4,256,256]{2,1,0:T(8,128)(2,1)S(1)}, u32[]{:S(2)}, u32[]{:S(2)}) collective-permute-start(bf16[4,256,256]{2,1,0:T(8,128)(2,1)S(1)} %pad_maximum_fusion.w0_ref), channel_id=1, source_target_pairs={{0,1},{1,0},{2,3},{3,2},{4,5},{5,4},{6,7},{7,6},{8,9},{9,8},{10,11... | collective-permute-start | bytes 1572872 | tf_op jit(solution)/shard_map/ppermute | solution.py:222
  80.0 4.7 %collective-permute-start.6 = (bf16[4,256,256]{2,1,0:T(8,128)(2,1)S(1)}, bf16[4,256,256]{2,1,0:T(8,128)(2,1)S(1)}, u32[]{:S(2)}, u32[]{:S(2)}) collective-permute-start(bf16[4,256,256]{2,1,0:T(8,128)(2,1)S(1)} %pad_maximum_fusion.w0_ref), channel_id=1, source_target_pairs={{0,2},{1,3},{2,0},{3,1},{4,6},{5,7},{6,4},{7,5},{8,10},{9,11},{10,... | collective-permute-start | bytes 1572872 | tf_op jit(solution)/shard_map/ppermute | solution.py:222
  84.7 3.8 %collective-permute-start.7 = (bf16[4,256,256]{2,1,0:T(8,128)(2,1)S(1)}, bf16[4,256,256]{2,1,0:T(8,128)(2,1)S(1)}, u32[]{:S(2)}, u32[]{:S(2)}) collective-permute-start(bf16[4,256,256]{2,1,0:T(8,128)(2,1)S(1)} %pad_maximum_fusion.w0_ref), channel_id=1, source_target_pairs={{0,3},{1,2},{2,1},{3,0},{4,7},{5,6},{6,5},{7,4},{8,11},{9,10},{10,... | collective-permute-start | bytes 1572872 | tf_op jit(solution)/shard_map/ppermute | solution.py:222
  88.5 0.1 pad_add_fusion.place_ref
  88.6 6.2 %collective-permute-done.5.w1_ref = bf16[4,256,256]{2,1,0:T(8,128)(2,1)S(1)} collective-permute-done((bf16[4,256,256]{2,1,0:T(8,128)(2,1)S(1)}, bf16[4,256,256]{2,1,0:T(8,128)(2,1)S(1)}, u32[]{:S(2)}, u32[]{:S(2)}) %collective-permute-start.5) | collective-permute-done | bytes 524320 | tf_op jit(solution)/shard_map/ppermute | solution.py:222
  94.7 11.1 %collective-permute-done.6.w2_ref = bf16[4,256,256]{2,1,0:T(8,128)(2,1)S(1)} collective-permute-done((bf16[4,256,256]{2,1,0:T(8,128)(2,1)S(1)}, bf16[4,256,256]{2,1,0:T(8,128)(2,1)S(1)}, u32[]{:S(2)}, u32[]{:S(2)}) %collective-permute-start.6) | collective-permute-done | bytes 524320 | tf_op jit(solution)/shard_map/ppermute | solution.py:222
  105.9 6.4 %collective-permute-done.7.w3_ref = bf16[4,256,256]{2,1,0:T(8,128)(2,1)S(1)} collective-permute-done((bf16[4,256,256]{2,1,0:T(8,128)(2,1)S(1)}, bf16[4,256,256]{2,1,0:T(8,128)(2,1)S(1)}, u32[]{:S(2)}, u32[]{:S(2)}) %collective-permute-start.7) | collective-permute-done | bytes 524320 | tf_op jit(solution)/shard_map/ppermute | solution.py:222
  112.3 0.0 all-to-all-done.2
  112.3 2.0 %project.1 = (f32[2,256,256]{2,1,0:T(8,128)S(1)}, f32[2,256,256]{2,1,0:T(8,128)}) custom-call(s32[3]{0:T(128)S(1)} %pad_add_fusion.place_ref, bf16[4,256,256]{2,1,0:T(8,128)(2,1)S(1)} %bitcast.19, bf16[4,256,256]{2,1,0:T(8,128)(2,1)S(1)} %pad_maximum_fusion.w0_ref, bf16[4,256,256]{2,1,0:T(8,128)(2,1)S(1)} %collective-permute-done.5.w1_ref, ...), custom_call_target="tpu_custom_call" | custom-call | flops 540000000 | bytes 4000000 | tf_op jit(solution)/shard_map/project/pallas_call | solution.py:209
  114.3 1.9 %collective-permute-start.8 = (f32[2,256,256]{2,1,0:T(8,128)}, f32[2,256,256]{2,1,0:T(8,128)S(1)}, u32[]{:S(2)}, u32[]{:S(2)}) collective-permute-start(f32[2,256,256]{2,1,0:T(8,128)} %get-tuple-element.8), channel_id=1, source_target_pairs={{0,16},{16,0},{1,17},{17,1},{2,18},{18,2},{3,19},{19,3},{4,20},{20... | collective-permute-start | bytes 1572872 | tf_op jit(solution)/shard_map/ppermute | solution.py:222
  116.3 2.1 %collective-permute-done.8 = f32[2,256,256]{2,1,0:T(8,128)S(1)} collective-permute-done((f32[2,256,256]{2,1,0:T(8,128)}, f32[2,256,256]{2,1,0:T(8,128)S(1)}, u32[]{:S(2)}, u32[]{:S(2)}) %collective-permute-start.8) | collective-permute-done | bytes 524320 | tf_op jit(solution)/shard_map/ppermute | solution.py:222
  118.3 0.1 add.27
  118.4 6.0 %collective-permute-start.9 = (bf16[256,256]{1,0:T(8,128)(2,1)S(1)}, bf16[256,256]{1,0:T(8,128)(2,1)S(1)}, u32[]{:S(2)}, u32[]{:S(2)}) collective-permute-start(bf16[256,256]{1,0:T(8,128)(2,1)S(1)} %fusion.1), channel_id=1, source_target_pairs={{0,256},{256,0},{1,257},{257,1},{2,258},{258,2},{3,259},{259,3},{4... | collective-permute-start | bytes 393224 | tf_op jit(solution)/shard_map/ppermute | solution.py:222
  124.5 8.1 %collective-permute-done.9 = bf16[256,256]{1,0:T(8,128)(2,1)S(1)} collective-permute-done((bf16[256,256]{1,0:T(8,128)(2,1)S(1)}, bf16[256,256]{1,0:T(8,128)(2,1)S(1)}, u32[]{:S(2)}, u32[]{:S(2)}) %collective-permute-start.9) | collective-permute-done | bytes 131104 | tf_op jit(solution)/shard_map/ppermute | solution.py:222
  132.6 0.7 fusion
  (4 shorter events, 0.1 us)
Async XLA Ops:
  0.0 3.4 %copy-start = (bf16[4,128,8]{1,2,0:T(8,128)(2,1)S(1)}, bf16[4,128,8]{1,2,0:T(8,128)(2,1)}, u32[]{:S(2)}) copy-start(bf16[4,128,8]{1,2,0:T(8,128)(2,1)} %param.4) | copy-start | bytes 24580
  0.0 3.4 %collective-permute-start.1 = (bf16[4,8,128]{2,1,0:T(8,128)(2,1)}, bf16[4,8,128]{2,1,0:T(8,128)(2,1)S(1)}, u32[]{:S(2)}, u32[]{:S(2)}) collective-permute-start(bf16[4,8,128]{2,1,0:T(8,128)(2,1)} %bitcast.25), channel_id=1, source_target_pairs={{0,16},{16,0},{1,17},{17,1},{2,18},{18,2},{3,19},{19,3},{4,20},{20... | collective-permute-start | bytes 24584 | tf_op jit(solution)/shard_map/ppermute | solution.py:222
  4.2 26.2 %all-to-all-start = ((bf16[16,2,4,8,128]{4,3,2,1,0:T(8,128)(2,1)}), bf16[16,2,4,8,128]{4,3,2,1,0:T(8,128)(2,1)S(1)}, u32[]{:S(2)}, u32[]{:S(2)}) async-start(bf16[16,2,4,8,128]{4,3,2,1,0:T(8,128)(2,1)} %broadcast_in_dim.2), calls=%async_computation | async-start | bytes 524288 | tf_op jit(solution)/shard_map/all_to_all | solution.py:234
  31.2 6.8 %copy-start.1 = (bf16[256,256]{1,0:T(8,128)(2,1)S(1)}, bf16[256,256]{1,0:T(8,128)(2,1)}, u32[]{:S(2)}) copy-start(bf16[256,256]{1,0:T(8,128)(2,1)} %param.5) | copy-start | bytes 393220
  31.2 16.4 %copy-start.2 = (bf16[128,256]{1,0:T(8,128)(2,1)S(1)}, bf16[128,256]{1,0:T(8,128)(2,1)}, u32[]{:S(2)}) copy-start(bf16[128,256]{1,0:T(8,128)(2,1)} %param.3) | copy-start | bytes 196612
  31.2 28.9 %all-to-all-start.1 = ((bf16[16,112,128]{2,1,0:T(8,128)(2,1)}), bf16[16,112,128]{2,1,0:T(8,128)(2,1)S(1)}, u32[]{:S(2)}, u32[]{:S(2)}) async-start(bf16[16,112,128]{2,1,0:T(8,128)(2,1)} %windows.1), calls=%async_computation.1 | async-start | bytes 917504 | tf_op jit(solution)/shard_map/all_to_all | solution.py:242
  38.0 10.2 %collective-permute-start.2 = (bf16[256,256]{1,0:T(8,128)(2,1)S(1)}, bf16[256,256]{1,0:T(8,128)(2,1)S(1)}, u32[]{:S(2)}, u32[]{:S(2)}) collective-permute-start(bf16[256,256]{1,0:T(8,128)(2,1)S(1)} %copy-done.1), channel_id=1, source_target_pairs={{0,0},{1,1},{2,2},{3,3},{4,16},{5,17},{6,18},{7,19},{8,256},{9,257... | collective-permute-start | bytes 393224 | tf_op jit(solution)/shard_map/ppermute | solution.py:229
  38.7 19.0 %collective-permute-start.3 = (bf16[256,256]{1,0:T(8,128)(2,1)S(1)}, bf16[256,256]{1,0:T(8,128)(2,1)S(1)}, u32[]{:S(2)}, u32[]{:S(2)}) collective-permute-start(bf16[256,256]{1,0:T(8,128)(2,1)S(1)} %copy-done.1), channel_id=1, source_target_pairs={{0,8},{1,9},{2,10},{3,11},{4,24},{5,25},{6,26},{7,27},{8,264},{9,2... | collective-permute-start | bytes 393224 | tf_op jit(solution)/shard_map/ppermute | solution.py:235
  47.5 12.5 %collective-permute-start = (bf16[128,256]{1,0:T(8,128)(2,1)S(1)}, bf16[128,256]{1,0:T(8,128)(2,1)S(1)}, u32[]{:S(2)}, u32[]{:S(2)}) collective-permute-start(bf16[128,256]{1,0:T(8,128)(2,1)S(1)} %copy-done.2), channel_id=1, source_target_pairs={{0,0},{1,64},{2,128},{3,192},{4,16},{5,80},{6,144},{7,208},{8,256}... | collective-permute-start | bytes 196616 | tf_op jit(solution)/shard_map/ppermute | solution.py:230
  57.7 20.3 %collective-permute-start.4 = (bf16[2,256,256]{2,1,0:T(8,128)(2,1)S(1)}, bf16[2,256,256]{2,1,0:T(8,128)(2,1)S(1)}, u32[]{:S(2)}, u32[]{:S(2)}) collective-permute-start(bf16[2,256,256]{2,1,0:T(8,128)(2,1)S(1)} %pad_maximum_fusion.1), channel_id=1, source_target_pairs={{0,4},{4,0},{8,12},{12,8},{1,5},{5,1},{9,13},{13,9},{2,6},{6,2},{1... | collective-permute-start | bytes 786440 | tf_op jit(solution)/shard_map/ppermute | solution.py:222
  70.5 41.8 %all-to-all-start.2 = ((bf16[8,128,256]{2,1,0:T(8,128)(2,1)}), bf16[8,128,256]{2,1,0:T(8,128)(2,1)S(1)}, u32[]{:S(2)}, u32[]{:S(2)}) async-start(bf16[8,128,256]{2,1,0:T(8,128)(2,1)} %attend.1), calls=%async_computation.2 | async-start | bytes 1048576 | tf_op jit(solution)/shard_map/all_to_all | solution.py:244
  78.0 16.7 %collective-permute-start.5 = (bf16[4,256,256]{2,1,0:T(8,128)(2,1)S(1)}, bf16[4,256,256]{2,1,0:T(8,128)(2,1)S(1)}, u32[]{:S(2)}, u32[]{:S(2)}) collective-permute-start(bf16[4,256,256]{2,1,0:T(8,128)(2,1)S(1)} %pad_maximum_fusion.w0_ref), channel_id=1, source_target_pairs={{0,1},{1,0},{2,3},{3,2},{4,5},{5,4},{6,7},{7,6},{8,9},{9,8},{10,11... | collective-permute-start | bytes 1572872 | tf_op jit(solution)/shard_map/ppermute | solution.py:222
  80.0 25.9 %collective-permute-start.6 = (bf16[4,256,256]{2,1,0:T(8,128)(2,1)S(1)}, bf16[4,256,256]{2,1,0:T(8,128)(2,1)S(1)}, u32[]{:S(2)}, u32[]{:S(2)}) collective-permute-start(bf16[4,256,256]{2,1,0:T(8,128)(2,1)S(1)} %pad_maximum_fusion.w0_ref), channel_id=1, source_target_pairs={{0,2},{1,3},{2,0},{3,1},{4,6},{5,7},{6,4},{7,5},{8,10},{9,11},{10,... | collective-permute-start | bytes 1572872 | tf_op jit(solution)/shard_map/ppermute | solution.py:222
  84.7 27.6 %collective-permute-start.7 = (bf16[4,256,256]{2,1,0:T(8,128)(2,1)S(1)}, bf16[4,256,256]{2,1,0:T(8,128)(2,1)S(1)}, u32[]{:S(2)}, u32[]{:S(2)}) collective-permute-start(bf16[4,256,256]{2,1,0:T(8,128)(2,1)S(1)} %pad_maximum_fusion.w0_ref), channel_id=1, source_target_pairs={{0,3},{1,2},{2,1},{3,0},{4,7},{5,6},{6,5},{7,4},{8,11},{9,10},{10,... | collective-permute-start | bytes 1572872 | tf_op jit(solution)/shard_map/ppermute | solution.py:222
  114.3 4.0 %collective-permute-start.8 = (f32[2,256,256]{2,1,0:T(8,128)}, f32[2,256,256]{2,1,0:T(8,128)S(1)}, u32[]{:S(2)}, u32[]{:S(2)}) collective-permute-start(f32[2,256,256]{2,1,0:T(8,128)} %get-tuple-element.8), channel_id=1, source_target_pairs={{0,16},{16,0},{1,17},{17,1},{2,18},{18,2},{3,19},{19,3},{4,20},{20... | collective-permute-start | bytes 1572872 | tf_op jit(solution)/shard_map/ppermute | solution.py:222
  118.4 14.1 %collective-permute-start.9 = (bf16[256,256]{1,0:T(8,128)(2,1)S(1)}, bf16[256,256]{1,0:T(8,128)(2,1)S(1)}, u32[]{:S(2)}, u32[]{:S(2)}) collective-permute-start(bf16[256,256]{1,0:T(8,128)(2,1)S(1)} %fusion.1), channel_id=1, source_target_pairs={{0,256},{256,0},{1,257},{257,1},{2,258},{258,2},{3,259},{259,3},{4... | collective-permute-start | bytes 393224 | tf_op jit(solution)/shard_map/ppermute | solution.py:222

commit v6 on v5

--- a/solution.py
+++ b/solution.py
@@ -202,13 +202,13 @@
             if slot == 0:
                 keep_ref[half] = total
             else:
-                send_ref[half] = total
+                send_ref[half] = total.astype(BF16)
 
 
 def project(place, attention, weights):
     return pl.pallas_call(
         project_kernel,
-        out_shape=(jax.ShapeDtypeStruct((2, 256, 256), F32), jax.ShapeDtypeStruct((2, 256, 256), F32)),
+        out_shape=(jax.ShapeDtypeStruct((2, 256, 256), F32), jax.ShapeDtypeStruct((2, 256, 256), BF16)),
         in_specs=[pl.BlockSpec(memory_space=pltpu.SMEM)] + [pl.BlockSpec(memory_space=pltpu.VMEM)] * 5,
         out_specs=(pl.BlockSpec(memory_space=pltpu.VMEM), pl.BlockSpec(memory_space=pltpu.VMEM)),
         cost_estimate=pl.CostEstimate(flops=540_000_000, bytes_accessed=4_000_000, transcendentals=0),
@@ -244,7 +244,7 @@
     attention = lax.all_to_all(attention, "z", 0, 0)
     keep, send = project(jnp.stack([core, yl, x]), attention.reshape(4, 256, 256), weights)
     got = across(send, "core", 1)
-    summed = keep + got
+    summed = keep + got.astype(F32)
     leaving = lax.dynamic_index_in_dim(summed, 1 - yh, 0, keepdims=False).astype(BF16)
     arrived = across(leaving, "yh", 1)
     staying = lax.dynamic_index_in_dim(summed, yh, 0, keepdims=False)

time: 134 us -> 133 us (level)
  no operation moved by 1% of the time
where the time goes in v6:
time: 133 us; the launch traced here: 132 us
  starting transfers between devices  62.9 us (47%)
  waiting for transfers between devices  54.6 us (41%)
  Pallas kernels  12.5 us (9%)
    ppermute x7, waiting for transfers between devices, across(): return lax.ppermute(x, axis, [(i, i ^ away) for i in range(count)])  34.7 us
    ppermute x7, starting transfers between devices, across(): return lax.ppermute(x, axis, [(i, i ^ away) for i in range(count)])  22.7 us
    all_to_all x1, starting transfers between devices, layer(): lax.all_to_all(jnp.broadcast_to(pair[None], (16,) + pair.shape), ('yh', '...  15.7 us
    pallas_call x1, Pallas kernels, attend(): pl.pallas_call(attend_kernel, out_shape=jax.ShapeDtypeStruct((8, BLOCK, 2...  10.5 us
    all_to_all x1, waiting for transfers between devices, layer(): lax.all_to_all(jnp.broadcast_to(pair[None], (16,) + pair.shape), ('yh', '...  10.5 us
    ppermute x1, waiting for transfers between devices, layer(): columns = jnp.stack([moved, lax.ppermute(w_out, ALL, weight_pairs(2))])  9.42 us
    ppermute x1, starting transfers between devices, layer(): columns = jnp.stack([moved, lax.ppermute(w_out, ALL, weight_pairs(2))])  8.85 us
    all_to_all x1, starting transfers between devices, layer(): attention = lax.all_to_all(attention, 'z', 0, 0)  7.43 us
  transfers between devices with their start and end apart: 13, of which 8 were waited for; matrix products, arithmetic and copies ran while one was open for 0% of the time, Pallas kernels for 8%

profile of v6, /device:TPU:48, one launch (start us, length us, event | category | flops | bytes accessed | tf_op | source)
XLA Modules:
  0.0 131.9 jit_solution(1454541330716033745)
XLA Ops:
  0.0 0.0 copy-start
  0.0 2.0 %collective-permute-start.1 = (bf16[4,8,128]{2,1,0:T(8,128)(2,1)}, bf16[4,8,128]{2,1,0:T(8,128)(2,1)S(1)}, u32[]{:S(2)}, u32[]{:S(2)}) collective-permute-start(bf16[4,8,128]{2,1,0:T(8,128)(2,1)} %bitcast.25), channel_id=1, source_target_pairs={{0,16},{16,0},{1,17},{17,1},{2,18},{18,2},{3,19},{19,3},{4,20},{20... | collective-permute-start | bytes 24584 | tf_op jit(solution)/shard_map/ppermute | solution.py:222
  2.1 1.3 %collective-permute-done.1 = bf16[4,8,128]{2,1,0:T(8,128)(2,1)S(1)} collective-permute-done((bf16[4,8,128]{2,1,0:T(8,128)(2,1)}, bf16[4,8,128]{2,1,0:T(8,128)(2,1)S(1)}, u32[]{:S(2)}, u32[]{:S(2)}) %collective-permute-start.1) | collective-permute-done | bytes 8224 | tf_op jit(solution)/shard_map/ppermute | solution.py:222
  3.4 0.0 copy-done
  3.4 0.8 broadcast_in_dim.2
  4.2 15.7 %all-to-all-start = ((bf16[16,2,4,8,128]{4,3,2,1,0:T(8,128)(2,1)}), bf16[16,2,4,8,128]{4,3,2,1,0:T(8,128)(2,1)S(1)}, u32[]{:S(2)}, u32[]{:S(2)}) async-start(bf16[16,2,4,8,128]{4,3,2,1,0:T(8,128)(2,1)} %broadcast_in_dim.2), calls=%async_computation | async-start | bytes 524288 | tf_op jit(solution)/shard_map/all_to_all | solution.py:234
  19.9 10.5 %all-to-all-done = bf16[16,2,4,8,128]{4,3,2,1,0:T(8,128)(2,1)S(1)} async-done(((bf16[16,2,4,8,128]{4,3,2,1,0:T(8,128)(2,1)}), bf16[16,2,4,8,128]{4,3,2,1,0:T(8,128)(2,1)S(1)}, u32[]{:S(2)}, u32[]{:S(2)}) %all-to-all-start) | async-done | bytes 262176 | tf_op jit(solution)/shard_map/all_to_all | solution.py:234
  30.3 0.8 windows.1
  31.2 0.0 copy-start.1
  31.2 0.0 copy-start.2
  31.2 6.8 %all-to-all-start.1 = ((bf16[16,112,128]{2,1,0:T(8,128)(2,1)}), bf16[16,112,128]{2,1,0:T(8,128)(2,1)S(1)}, u32[]{:S(2)}, u32[]{:S(2)}) async-start(bf16[16,112,128]{2,1,0:T(8,128)(2,1)} %windows.1), calls=%async_computation.1 | async-start | bytes 917504 | tf_op jit(solution)/shard_map/all_to_all | solution.py:242
  38.0 0.0 copy-done.1
  38.0 0.7 collective-permute-start.2
  38.7 8.8 %collective-permute-start.3 = (bf16[256,256]{1,0:T(8,128)(2,1)S(1)}, bf16[256,256]{1,0:T(8,128)(2,1)S(1)}, u32[]{:S(2)}, u32[]{:S(2)}) collective-permute-start(bf16[256,256]{1,0:T(8,128)(2,1)S(1)} %copy-done.1), channel_id=1, source_target_pairs={{0,8},{1,9},{2,10},{3,11},{4,24},{5,25},{6,26},{7,27},{8,264},{9,2... | collective-permute-start | bytes 393224 | tf_op jit(solution)/shard_map/ppermute | solution.py:235
  47.5 0.0 copy-done.2
  47.5 0.7 collective-permute-start
  48.2 0.0 collective-permute-done.2
  48.2 9.4 %collective-permute-done.3 = bf16[256,256]{1,0:T(8,128)(2,1)S(1)} collective-permute-done((bf16[256,256]{1,0:T(8,128)(2,1)S(1)}, bf16[256,256]{1,0:T(8,128)(2,1)S(1)}, u32[]{:S(2)}, u32[]{:S(2)}) %collective-permute-start.3) | collective-permute-done | bytes 131104 | tf_op jit(solution)/shard_map/ppermute | solution.py:235
  57.7 2.4 %collective-permute-start.4 = (bf16[2,256,256]{2,1,0:T(8,128)(2,1)S(1)}, bf16[2,256,256]{2,1,0:T(8,128)(2,1)S(1)}, u32[]{:S(2)}, u32[]{:S(2)}) collective-permute-start(bf16[2,256,256]{2,1,0:T(8,128)(2,1)S(1)} %pad_maximum_fusion.1), channel_id=1, source_target_pairs={{0,4},{4,0},{8,12},{12,8},{1,5},{5,1},{9,13},{13,9},{2,6},{6,2},{1... | collective-permute-start | bytes 786440 | tf_op jit(solution)/shard_map/ppermute | solution.py:222
  60.0 0.0 collective-permute-done.q_ref
  60.0 0.0 all-to-all-done.1.kv_ref
  60.1 10.5 %attend.1 = bf16[8,128,256]{2,1,0:T(8,128)(2,1)} custom-call(s32[1]{0:T(128)} %bitcast.3.where_ref, bf16[128,256]{1,0:T(8,128)(2,1)S(1)} %collective-permute-done.q_ref, bf16[16,112,128]{2,1,0:T(8,128)(2,1)S(1)} %all-to-all-done.1.kv_ref), custom_call_target="tpu_custom_call" | custom-call | flops 6000000000 | bytes 1000000 | tf_op jit(solution)/shard_map/attend/pallas_call | solution.py:167
  70.5 7.4 %all-to-all-start.2 = ((bf16[8,128,256]{2,1,0:T(8,128)(2,1)}), bf16[8,128,256]{2,1,0:T(8,128)(2,1)S(1)}, u32[]{:S(2)}, u32[]{:S(2)}) async-start(bf16[8,128,256]{2,1,0:T(8,128)(2,1)} %attend.1), calls=%async_computation.2 | async-start | bytes 1048576 | tf_op jit(solution)/shard_map/all_to_all | solution.py:244
  77.9 0.0 collective-permute-done.4
  78.0 0.1 pad_maximum_fusion.w0_ref
  78.0 1.9 %collective-permute-start.5 = (bf16[4,256,256]{2,1,0:T(8,128)(2,1)S(1)}, bf16[4,256,256]{2,1,0:T(8,128)(2,1)S(1)}, u32[]{:S(2)}, u32[]{:S(2)}) collective-permute-start(bf16[4,256,256]{2,1,0:T(8,128)(2,1)S(1)} %pad_maximum_fusion.w0_ref), channel_id=1, source_target_pairs={{0,1},{1,0},{2,3},{3,2},{4,5},{5,4},{6,7},{7,6},{8,9},{9,8},{10,11... | collective-permute-start | bytes 1572872 | tf_op jit(solution)/shard_map/ppermute | solution.py:222
  80.0 4.7 %collective-permute-start.6 = (bf16[4,256,256]{2,1,0:T(8,128)(2,1)S(1)}, bf16[4,256,256]{2,1,0:T(8,128)(2,1)S(1)}, u32[]{:S(2)}, u32[]{:S(2)}) collective-permute-start(bf16[4,256,256]{2,1,0:T(8,128)(2,1)S(1)} %pad_maximum_fusion.w0_ref), channel_id=1, source_target_pairs={{0,2},{1,3},{2,0},{3,1},{4,6},{5,7},{6,4},{7,5},{8,10},{9,11},{10,... | collective-permute-start | bytes 1572872 | tf_op jit(solution)/shard_map/ppermute | solution.py:222
  84.7 3.8 %collective-permute-start.7 = (bf16[4,256,256]{2,1,0:T(8,128)(2,1)S(1)}, bf16[4,256,256]{2,1,0:T(8,128)(2,1)S(1)}, u32[]{:S(2)}, u32[]{:S(2)}) collective-permute-start(bf16[4,256,256]{2,1,0:T(8,128)(2,1)S(1)} %pad_maximum_fusion.w0_ref), channel_id=1, source_target_pairs={{0,3},{1,2},{2,1},{3,0},{4,7},{5,6},{6,5},{7,4},{8,11},{9,10},{10,... | collective-permute-start | bytes 1572872 | tf_op jit(solution)/shard_map/ppermute | solution.py:222
  88.5 0.1 pad_add_fusion.place_ref
  88.6 6.2 %collective-permute-done.5.w1_ref = bf16[4,256,256]{2,1,0:T(8,128)(2,1)S(1)} collective-permute-done((bf16[4,256,256]{2,1,0:T(8,128)(2,1)S(1)}, bf16[4,256,256]{2,1,0:T(8,128)(2,1)S(1)}, u32[]{:S(2)}, u32[]{:S(2)}) %collective-permute-start.5) | collective-permute-done | bytes 524320 | tf_op jit(solution)/shard_map/ppermute | solution.py:222
  94.7 11.1 %collective-permute-done.6.w2_ref = bf16[4,256,256]{2,1,0:T(8,128)(2,1)S(1)} collective-permute-done((bf16[4,256,256]{2,1,0:T(8,128)(2,1)S(1)}, bf16[4,256,256]{2,1,0:T(8,128)(2,1)S(1)}, u32[]{:S(2)}, u32[]{:S(2)}) %collective-permute-start.6) | collective-permute-done | bytes 524320 | tf_op jit(solution)/shard_map/ppermute | solution.py:222
  105.9 6.4 %collective-permute-done.7.w3_ref = bf16[4,256,256]{2,1,0:T(8,128)(2,1)S(1)} collective-permute-done((bf16[4,256,256]{2,1,0:T(8,128)(2,1)S(1)}, bf16[4,256,256]{2,1,0:T(8,128)(2,1)S(1)}, u32[]{:S(2)}, u32[]{:S(2)}) %collective-permute-start.7) | collective-permute-done | bytes 524320 | tf_op jit(solution)/shard_map/ppermute | solution.py:222
  112.3 0.0 all-to-all-done.2
  112.3 1.2 project.1
  113.6 1.9 %collective-permute-start.8 = (bf16[2,256,256]{2,1,0:T(8,128)(2,1)S(1)}, bf16[2,256,256]{2,1,0:T(8,128)(2,1)S(1)}, u32[]{:S(2)}, u32[]{:S(2)}) collective-permute-start(bf16[2,256,256]{2,1,0:T(8,128)(2,1)S(1)} %get-tuple-element.8), channel_id=1, source_target_pairs={{0,16},{16,0},{1,17},{17,1},{2,18},{18,2},{3,19},{19,3},{4,20},{20... | collective-permute-start | bytes 786440 | tf_op jit(solution)/shard_map/ppermute | solution.py:222
  115.5 1.5 %collective-permute-done.8 = bf16[2,256,256]{2,1,0:T(8,128)(2,1)S(1)} collective-permute-done((bf16[2,256,256]{2,1,0:T(8,128)(2,1)S(1)}, bf16[2,256,256]{2,1,0:T(8,128)(2,1)S(1)}, u32[]{:S(2)}, u32[]{:S(2)}) %collective-permute-start.8) | collective-permute-done | bytes 262176 | tf_op jit(solution)/shard_map/ppermute | solution.py:222
  117.0 0.1 convert_add_fusion
  117.1 6.0 %collective-permute-start.9 = (bf16[256,256]{1,0:T(8,128)(2,1)S(1)}, bf16[256,256]{1,0:T(8,128)(2,1)S(1)}, u32[]{:S(2)}, u32[]{:S(2)}) collective-permute-start(bf16[256,256]{1,0:T(8,128)(2,1)S(1)} %fusion.1), channel_id=1, source_target_pairs={{0,256},{256,0},{1,257},{257,1},{2,258},{258,2},{3,259},{259,3},{4... | collective-permute-start | bytes 393224 | tf_op jit(solution)/shard_map/ppermute | solution.py:222
  123.1 8.1 %collective-permute-done.9 = bf16[256,256]{1,0:T(8,128)(2,1)S(1)} collective-permute-done((bf16[256,256]{1,0:T(8,128)(2,1)S(1)}, bf16[256,256]{1,0:T(8,128)(2,1)S(1)}, u32[]{:S(2)}, u32[]{:S(2)}) %collective-permute-start.9) | collective-permute-done | bytes 131104 | tf_op jit(solution)/shard_map/ppermute | solution.py:222
  131.2 0.7 fusion
  (4 shorter events, 0.1 us)
Async XLA Ops:
  0.0 3.4 %copy-start = (bf16[4,128,8]{1,2,0:T(8,128)(2,1)S(1)}, bf16[4,128,8]{1,2,0:T(8,128)(2,1)}, u32[]{:S(2)}) copy-start(bf16[4,128,8]{1,2,0:T(8,128)(2,1)} %param.4) | copy-start | bytes 24580
  0.0 3.4 %collective-permute-start.1 = (bf16[4,8,128]{2,1,0:T(8,128)(2,1)}, bf16[4,8,128]{2,1,0:T(8,128)(2,1)S(1)}, u32[]{:S(2)}, u32[]{:S(2)}) collective-permute-start(bf16[4,8,128]{2,1,0:T(8,128)(2,1)} %bitcast.25), channel_id=1, source_target_pairs={{0,16},{16,0},{1,17},{17,1},{2,18},{18,2},{3,19},{19,3},{4,20},{20... | collective-permute-start | bytes 24584 | tf_op jit(solution)/shard_map/ppermute | solution.py:222
  4.2 26.2 %all-to-all-start = ((bf16[16,2,4,8,128]{4,3,2,1,0:T(8,128)(2,1)}), bf16[16,2,4,8,128]{4,3,2,1,0:T(8,128)(2,1)S(1)}, u32[]{:S(2)}, u32[]{:S(2)}) async-start(bf16[16,2,4,8,128]{4,3,2,1,0:T(8,128)(2,1)} %broadcast_in_dim.2), calls=%async_computation | async-start | bytes 524288 | tf_op jit(solution)/shard_map/all_to_all | solution.py:234
  31.2 6.8 %copy-start.1 = (bf16[256,256]{1,0:T(8,128)(2,1)S(1)}, bf16[256,256]{1,0:T(8,128)(2,1)}, u32[]{:S(2)}) copy-start(bf16[256,256]{1,0:T(8,128)(2,1)} %param.5) | copy-start | bytes 393220
  31.2 16.4 %copy-start.2 = (bf16[128,256]{1,0:T(8,128)(2,1)S(1)}, bf16[128,256]{1,0:T(8,128)(2,1)}, u32[]{:S(2)}) copy-start(bf16[128,256]{1,0:T(8,128)(2,1)} %param.3) | copy-start | bytes 196612
  31.2 28.9 %all-to-all-start.1 = ((bf16[16,112,128]{2,1,0:T(8,128)(2,1)}), bf16[16,112,128]{2,1,0:T(8,128)(2,1)S(1)}, u32[]{:S(2)}, u32[]{:S(2)}) async-start(bf16[16,112,128]{2,1,0:T(8,128)(2,1)} %windows.1), calls=%async_computation.1 | async-start | bytes 917504 | tf_op jit(solution)/shard_map/all_to_all | solution.py:242
  38.0 10.2 %collective-permute-start.2 = (bf16[256,256]{1,0:T(8,128)(2,1)S(1)}, bf16[256,256]{1,0:T(8,128)(2,1)S(1)}, u32[]{:S(2)}, u32[]{:S(2)}) collective-permute-start(bf16[256,256]{1,0:T(8,128)(2,1)S(1)} %copy-done.1), channel_id=1, source_target_pairs={{0,0},{1,1},{2,2},{3,3},{4,16},{5,17},{6,18},{7,19},{8,256},{9,257... | collective-permute-start | bytes 393224 | tf_op jit(solution)/shard_map/ppermute | solution.py:229
  38.7 19.0 %collective-permute-start.3 = (bf16[256,256]{1,0:T(8,128)(2,1)S(1)}, bf16[256,256]{1,0:T(8,128)(2,1)S(1)}, u32[]{:S(2)}, u32[]{:S(2)}) collective-permute-start(bf16[256,256]{1,0:T(8,128)(2,1)S(1)} %copy-done.1), channel_id=1, source_target_pairs={{0,8},{1,9},{2,10},{3,11},{4,24},{5,25},{6,26},{7,27},{8,264},{9,2... | collective-permute-start | bytes 393224 | tf_op jit(solution)/shard_map/ppermute | solution.py:235
  47.5 12.5 %collective-permute-start = (bf16[128,256]{1,0:T(8,128)(2,1)S(1)}, bf16[128,256]{1,0:T(8,128)(2,1)S(1)}, u32[]{:S(2)}, u32[]{:S(2)}) collective-permute-start(bf16[128,256]{1,0:T(8,128)(2,1)S(1)} %copy-done.2), channel_id=1, source_target_pairs={{0,0},{1,64},{2,128},{3,192},{4,16},{5,80},{6,144},{7,208},{8,256}... | collective-permute-start | bytes 196616 | tf_op jit(solution)/shard_map/ppermute | solution.py:230
  57.7 20.3 %collective-permute-start.4 = (bf16[2,256,256]{2,1,0:T(8,128)(2,1)S(1)}, bf16[2,256,256]{2,1,0:T(8,128)(2,1)S(1)}, u32[]{:S(2)}, u32[]{:S(2)}) collective-permute-start(bf16[2,256,256]{2,1,0:T(8,128)(2,1)S(1)} %pad_maximum_fusion.1), channel_id=1, source_target_pairs={{0,4},{4,0},{8,12},{12,8},{1,5},{5,1},{9,13},{13,9},{2,6},{6,2},{1... | collective-permute-start | bytes 786440 | tf_op jit(solution)/shard_map/ppermute | solution.py:222
  70.5 41.8 %all-to-all-start.2 = ((bf16[8,128,256]{2,1,0:T(8,128)(2,1)}), bf16[8,128,256]{2,1,0:T(8,128)(2,1)S(1)}, u32[]{:S(2)}, u32[]{:S(2)}) async-start(bf16[8,128,256]{2,1,0:T(8,128)(2,1)} %attend.1), calls=%async_computation.2 | async-start | bytes 1048576 | tf_op jit(solution)/shard_map/all_to_all | solution.py:244
  78.0 16.7 %collective-permute-start.5 = (bf16[4,256,256]{2,1,0:T(8,128)(2,1)S(1)}, bf16[4,256,256]{2,1,0:T(8,128)(2,1)S(1)}, u32[]{:S(2)}, u32[]{:S(2)}) collective-permute-start(bf16[4,256,256]{2,1,0:T(8,128)(2,1)S(1)} %pad_maximum_fusion.w0_ref), channel_id=1, source_target_pairs={{0,1},{1,0},{2,3},{3,2},{4,5},{5,4},{6,7},{7,6},{8,9},{9,8},{10,11... | collective-permute-start | bytes 1572872 | tf_op jit(solution)/shard_map/ppermute | solution.py:222
  80.0 25.9 %collective-permute-start.6 = (bf16[4,256,256]{2,1,0:T(8,128)(2,1)S(1)}, bf16[4,256,256]{2,1,0:T(8,128)(2,1)S(1)}, u32[]{:S(2)}, u32[]{:S(2)}) collective-permute-start(bf16[4,256,256]{2,1,0:T(8,128)(2,1)S(1)} %pad_maximum_fusion.w0_ref), channel_id=1, source_target_pairs={{0,2},{1,3},{2,0},{3,1},{4,6},{5,7},{6,4},{7,5},{8,10},{9,11},{10,... | collective-permute-start | bytes 1572872 | tf_op jit(solution)/shard_map/ppermute | solution.py:222
  84.7 27.6 %collective-permute-start.7 = (bf16[4,256,256]{2,1,0:T(8,128)(2,1)S(1)}, bf16[4,256,256]{2,1,0:T(8,128)(2,1)S(1)}, u32[]{:S(2)}, u32[]{:S(2)}) collective-permute-start(bf16[4,256,256]{2,1,0:T(8,128)(2,1)S(1)} %pad_maximum_fusion.w0_ref), channel_id=1, source_target_pairs={{0,3},{1,2},{2,1},{3,0},{4,7},{5,6},{6,5},{7,4},{8,11},{9,10},{10,... | collective-permute-start | bytes 1572872 | tf_op jit(solution)/shard_map/ppermute | solution.py:222
  113.6 3.4 %collective-permute-start.8 = (bf16[2,256,256]{2,1,0:T(8,128)(2,1)S(1)}, bf16[2,256,256]{2,1,0:T(8,128)(2,1)S(1)}, u32[]{:S(2)}, u32[]{:S(2)}) collective-permute-start(bf16[2,256,256]{2,1,0:T(8,128)(2,1)S(1)} %get-tuple-element.8), channel_id=1, source_target_pairs={{0,16},{16,0},{1,17},{17,1},{2,18},{18,2},{3,19},{19,3},{4,20},{20... | collective-permute-start | bytes 786440 | tf_op jit(solution)/shard_map/ppermute | solution.py:222
  117.1 14.1 %collective-permute-start.9 = (bf16[256,256]{1,0:T(8,128)(2,1)S(1)}, bf16[256,256]{1,0:T(8,128)(2,1)S(1)}, u32[]{:S(2)}, u32[]{:S(2)}) collective-permute-start(bf16[256,256]{1,0:T(8,128)(2,1)S(1)} %fusion.1), channel_id=1, source_target_pairs={{0,256},{256,0},{1,257},{257,1},{2,258},{258,2},{3,259},{259,3},{4... | collective-permute-start | bytes 393224 | tf_op jit(solution)/shard_map/ppermute | solution.py:222
